TPU v7x, 128 devices: a whole 4x4x4 slice. The times are simulated.
128 devices in a mesh: seq: 32 (over z, x, core), tp: 4 (over y).
Axes of the slice: x: 4, y: 4, z: 4, core: 2. Of those that a mesh axis runs over, the one named last changes fastest.
Arguments:
- hidden: bfloat16 [32, 4, 2048], P(None, None, 'seq'), may hold values from -6 to 6
- embedded: bfloat16 [32, 4, 2048], P(None, None, 'seq'), may hold values from -6 to 6
- request_group: int32 [32], replicated, may hold values from 0 to 7, as said below
- group_prompt_length: int32 [8], replicated, may hold values from 1 to 4096, as said below
- prompt_key_cache: bfloat16 [8, 4096, 4096], P(None, 'seq', 'tp'), may hold values from -500 to 500
- prompt_value_cache: bfloat16 [8, 4096, 4096], P(None, 'seq', 'tp'), may hold values from -6 to 6
- input_norm_gain: float32 [2, 2048], P(None, 'seq'), may hold values from 0.25 to 1.75
- query_key_value_weight: bfloat16 [3, 2, 2048, 4096], P(None, None, 'seq', 'tp'), may hold values from -0.09375 to 0.09375
- attention_output_weight: bfloat16 [4096, 2048], P('tp', 'seq'), may hold values from -0.09375 to 0.09375
- middle_norm_gain: float32 [2048], P('seq'), may hold values from 0.25 to 1.75
- gate_up_weight: bfloat16 [2, 2048, 8192], P(None, 'seq', 'tp'), may hold values from -0.125 to 0.125
- adapter_down_weight: bfloat16 [2048, 128], P('seq'), may hold values from -0.125 to 0.125
- adapter_up_weight: bfloat16 [128, 2, 8192], P(None, None, 'tp'), may hold values from -0.5 to 0.5
- down_weight: bfloat16 [8192, 2048], P('tp', 'seq'), may hold values from -0.0625 to 0.0625
- mamba_norm_gain: float32 [2048], P('seq'), may hold values from 0.25 to 1.75
- input_gate_x_weight: bfloat16 [2, 2048, 4096], P(None, 'seq', 'tp'), may hold values from -0.125 to 0.125
- input_step_weight: bfloat16 [2048, 64], P('seq', 'tp'), may hold values from -0.125 to 0.125
- input_bc_weight: bfloat16 [2048, 128], P('seq'), may hold values from -0.125 to 0.125
- convolution_x_taps: float32 [4, 4096], P(None, 'tp'), may hold values from -3 to 3
- convolution_bc_taps: float32 [4, 128], replicated, may hold values from -3 to 3
- prompt_tail_x: bfloat16 [32, 3, 4096], P('seq', None, 'tp'), may hold values from -6 to 6
- prompt_tail_bc: bfloat16 [32, 3, 128], P('seq'), may hold values from -6 to 6
- step_bias: float32 [64], P('tp'), may hold values from -3 to -0.5
- head_decay_rate: float32 [64], P('tp'), may hold values from 0.05 to 2
- head_skip_gain: float32 [64], P('tp'), may hold values from 0.5 to 2
- prompt_state: float32 [32, 64, 64, 64], P('seq', 'tp'), may hold values from -6 to 6
- gated_norm_gain: float32 [4096], P('tp'), may hold values from 0.25 to 1.75
- mamba_output_weight: bfloat16 [4096, 2048], P('tp', 'seq'), may hold values from -0.09375 to 0.09375
Outputs:
- layer_out: bfloat16 [32, 4, 2048], P(None, None, 'seq')
- updated_state: float32 [32, 64, 64, 64], P('seq', 'tp')
Inputs may be any that keep to these rules, and one draw needn't show every extreme that they name: `request_group`: every one of the 8 groups serves at least one request. `group_prompt_length`: some group's prompt fills all 4096 positions.
All inputs are finite; a program needn't handle non-finite values.
Results may differ from a plain program's by a relative error of at most 0.012.
The roundings to bfloat16 on the way count: a program that leaves them out, or rounds other values in their place, can miss the bound.
Values may be sent and summed in bfloat16 or wider, within the bound.
No kernel may reach another device: no remote copies, remote signals or barrier semaphores. Data moves between devices by JAX's collectives and lax.ppermute only.
A program may use at most 128 MiB of HBM per device.

v0:
```python
import math

import jax
import jax.numpy as jnp
from jax import lax
from jax.sharding import PartitionSpec as P

HD = 128
MAMBA_HEAD_SIZE = 64


EPS = 1e-05
HIGHEST = lax.Precision.HIGHEST
NEG_FILL = -1e30


def sequence_total(values):
    return lax.psum(values, "seq")


def tp_total(values):
    return lax.psum(values, "tp")


def row_shares(values):
    return (
        lax.psum_scatter(values[0], "seq", scatter_dimension=0, tiled=True),
        lax.psum_scatter(values[1], "seq", scatter_dimension=0, tiled=True),
        lax.psum_scatter(values[2], "seq", scatter_dimension=0, tiled=True),
    )


def row_gather(rows_part, weight):
    return jnp.dot(
        lax.all_gather(rows_part, "seq", axis=0, tiled=True),
        weight,
        preferred_element_type=jnp.float32,
    )


def apply_activation(partial_sums, adapter_low_rows, adapter_up_weight):
    adapter_low_narrow = adapter_low_rows.astype(jnp.bfloat16)
    gate_before = partial_sums[:, 0] + jnp.dot(
        adapter_low_narrow, adapter_up_weight[:, 0], preferred_element_type=jnp.float32
    )
    up_before = partial_sums[:, 1] + jnp.dot(
        adapter_low_narrow, adapter_up_weight[:, 1], preferred_element_type=jnp.float32
    )
    return (jax.nn.silu(gate_before) * up_before).astype(jnp.bfloat16)


def causal_conv(history, fresh, taps):
    joined = jnp.concatenate([history.astype(jnp.float32), fresh], axis=1)
    length = fresh.shape[1]
    result = jnp.zeros_like(fresh)
    for tap_index in range(taps.shape[0]):
        result = result + taps[tap_index] * joined[:, tap_index : tap_index + length]
    return jax.nn.silu(result)


def state_space_scan(
    state, inputs, b_mat, c_mat, step_length, decay_factor, head_skip_gain, head_dim
):
    requests, new_tok, channels = inputs.shape
    heads_count = channels // head_dim
    outputs = []
    for token_index in range(new_tok):
        per_head = inputs[:, token_index].reshape(requests, heads_count, head_dim)
        state = (
            decay_factor[:, token_index, :, None, None] * state
            + step_length[:, token_index, :, None, None]
            * per_head[..., None]
            * b_mat[:, token_index, None, None, :]
        )
        output = jnp.einsum("rhps,rs->rhp", state, c_mat[:, token_index], precision=HIGHEST)
        outputs.append(
            (output + head_skip_gain[None, :, None] * per_head).reshape(requests, channels)
        )
    return (state, jnp.stack(outputs, axis=1))


def on_device(
    hidden,
    embedded,
    request_group,
    group_prompt_length,
    prompt_key_cache,
    prompt_value_cache,
    input_norm_gain,
    query_key_value_weight,
    attention_output_weight,
    middle_norm_gain,
    gate_up_weight,
    adapter_down_weight,
    adapter_up_weight,
    down_weight,
    mamba_norm_gain,
    input_gate_x_weight,
    input_step_weight,
    input_bc_weight,
    convolution_x_taps,
    convolution_bc_taps,
    prompt_tail_x,
    prompt_tail_bc,
    step_bias,
    head_decay_rate,
    head_skip_gain,
    prompt_state,
    gated_norm_gain,
    mamba_output_weight,
):
    requests, new_tok, columns = hidden.shape
    rows = requests * new_tok
    width = columns * lax.axis_size("seq")
    hidden_rows = hidden.reshape(rows, columns).astype(jnp.float32)
    embed_rows = embedded.reshape(rows, columns).astype(jnp.float32)
    first_stat = sequence_total(
        jnp.sum(hidden_rows * hidden_rows, axis=1) + jnp.sum(embed_rows * embed_rows, axis=1)
    )
    first_factor = lax.rsqrt(first_stat / (2 * width) + EPS)[:, None]
    normed_hidden = (hidden_rows * first_factor * input_norm_gain[0]).astype(jnp.bfloat16)
    normed_embed = (embed_rows * first_factor * input_norm_gain[1]).astype(jnp.bfloat16)

    def body_project(which):
        return jnp.dot(
            normed_hidden, query_key_value_weight[which, 0], preferred_element_type=jnp.float32
        ) + jnp.dot(
            normed_embed, query_key_value_weight[which, 1], preferred_element_type=jnp.float32
        )

    query, new_keys, new_values = sequence_total(
        (body_project(0), body_project(1), body_project(2))
    )
    groups, cache_len, width_local = prompt_key_cache.shape
    heads_local = width_local // HD
    scale = 1.0 / math.sqrt(HD)
    query_heads = query.astype(jnp.bfloat16).reshape(rows, heads_local, HD)
    key_heads = new_keys.astype(jnp.bfloat16).reshape(rows, heads_local, HD)
    value_heads = new_values.astype(jnp.bfloat16).reshape(rows, heads_local, HD)
    row_ids = jnp.arange(rows)
    same_request = row_ids[:, None] // new_tok == row_ids[None, :] // new_tok
    earlier_token = row_ids[:, None] % new_tok >= row_ids[None, :] % new_tok
    self_mask = (same_request & earlier_token & (lax.axis_index("seq") == 0))[:, None, :]
    self_scores = (
        jnp.einsum("qhd,khd->qhk", query_heads, key_heads, preferred_element_type=jnp.float32)
        * scale
    )
    maxima = jnp.max(jnp.where(self_mask, self_scores, NEG_FILL), axis=-1)
    weights = jnp.where(self_mask, jnp.exp(self_scores - maxima[..., None]), 0.0)
    totals = jnp.sum(weights, axis=-1)
    accum = jnp.einsum("qhk,khd->qhd", weights, value_heads.astype(jnp.float32), precision=HIGHEST)
    row_group = jnp.repeat(request_group, new_tok)
    group_match = row_group[:, None] == jnp.arange(groups)[None, :]
    row_length = jnp.sum(jnp.where(group_match, group_prompt_length[None, :], 0), axis=1)
    block = math.gcd(cache_len, 32)
    start_dev = lax.axis_index("seq") * cache_len
    key_group = jnp.repeat(jnp.arange(groups), block)
    offsets = jnp.tile(jnp.arange(block), groups)
    key_match = row_group[:, None] == key_group[None, :]

    def cache_block(block_index, carry):
        old_max, old_total, old_accum = carry
        first_pos = block_index * block
        key_block = lax.dynamic_slice_in_dim(prompt_key_cache, first_pos, block, 1).reshape(
            groups * block, heads_local, HD
        )
        value_block = lax.dynamic_slice_in_dim(prompt_value_cache, first_pos, block, 1).reshape(
            groups * block, heads_local, HD
        )
        scores = (
            jnp.einsum("qhd,khd->qhk", query_heads, key_block, preferred_element_type=jnp.float32)
            * scale
        )
        positions = start_dev + first_pos + offsets
        mask = (key_match & (positions[None, :] < row_length[:, None]))[:, None, :]
        fresh_max = jnp.maximum(old_max, jnp.max(jnp.where(mask, scores, NEG_FILL), axis=-1))
        block_weights = jnp.where(mask, jnp.exp(scores - fresh_max[..., None]), 0.0)
        rescale = jnp.exp(old_max - fresh_max)
        new_total = old_total * rescale + jnp.sum(block_weights, axis=-1)
        new_accum = old_accum * rescale[..., None] + jnp.einsum(
            "qhk,khd->qhd", block_weights, value_block.astype(jnp.float32), precision=HIGHEST
        )
        return (fresh_max, new_total, new_accum)

    maxima, totals, accum = lax.fori_loop(
        0, cache_len // block, cache_block, (maxima, totals, accum)
    )
    top_score = lax.pmax(maxima, "seq")
    factor = jnp.exp(maxima - top_score)
    totals, accum = sequence_total((totals * factor, accum * factor[..., None]))
    attn = (accum / totals[..., None]).reshape(rows, width_local).astype(jnp.bfloat16)
    resid = hidden_rows + tp_total(
        jnp.dot(attn, attention_output_weight, preferred_element_type=jnp.float32)
    )
    mid_stat = sequence_total(jnp.sum(resid * resid, axis=1))
    middle_rows = (resid * lax.rsqrt(mid_stat / width + EPS)[:, None] * middle_norm_gain).astype(
        jnp.bfloat16
    )
    gate_and_up = jnp.stack(
        [
            jnp.dot(middle_rows, gate_up_weight[0], preferred_element_type=jnp.float32),
            jnp.dot(middle_rows, gate_up_weight[1], preferred_element_type=jnp.float32),
        ],
        axis=1,
    )
    adapter_low_rows = jnp.dot(middle_rows, adapter_down_weight, preferred_element_type=jnp.float32)
    gate_and_up, adapter_low_rows = sequence_total((gate_and_up, adapter_low_rows))
    activated_rows = apply_activation(gate_and_up, adapter_low_rows, adapter_up_weight)
    mlp_part = jnp.dot(activated_rows, down_weight, preferred_element_type=jnp.float32)
    block_out = resid + tp_total(mlp_part)
    mamba_stat = sequence_total(jnp.sum(block_out * block_out, axis=1))
    mamba_in = (block_out * lax.rsqrt(mamba_stat / width + EPS)[:, None] * mamba_norm_gain).astype(
        jnp.bfloat16
    )
    zx_parts = jnp.stack(
        [
            jnp.dot(mamba_in, input_gate_x_weight[0], preferred_element_type=jnp.float32),
            jnp.dot(mamba_in, input_gate_x_weight[1], preferred_element_type=jnp.float32),
        ],
        axis=1,
    )
    dt_raw = jnp.dot(mamba_in, input_step_weight, preferred_element_type=jnp.float32)
    bc_raw = jnp.dot(mamba_in, input_bc_weight, preferred_element_type=jnp.float32)
    zx_parts, dt_raw, bc_raw = row_shares((zx_parts, dt_raw, bc_raw))
    local_req = prompt_tail_x.shape[0]
    local_rows = local_req * new_tok
    inner_local = zx_parts.shape[2]
    zx_parts = zx_parts.reshape(local_req, new_tok, 2, inner_local)
    convolved_x = causal_conv(prompt_tail_x, zx_parts[:, :, 1], convolution_x_taps)
    convolved_bc = causal_conv(
        prompt_tail_bc, bc_raw.reshape(local_req, new_tok, bc_raw.shape[1]), convolution_bc_taps
    )
    state_dim = convolved_bc.shape[-1] // 2
    step_length = jax.nn.softplus(dt_raw.reshape(local_req, new_tok, dt_raw.shape[1]) + step_bias)
    decay_factor = jnp.exp(-step_length * head_decay_rate)
    updated_state, mamba_output = state_space_scan(
        prompt_state,
        convolved_x,
        convolved_bc[..., :state_dim],
        convolved_bc[..., state_dim:],
        step_length,
        decay_factor,
        head_skip_gain,
        MAMBA_HEAD_SIZE,
    )
    gated = mamba_output * jax.nn.silu(zx_parts[:, :, 0])
    gated_stat = tp_total(jnp.sum(gated * gated, axis=-1))
    inner_width = inner_local * lax.axis_size("tp")
    normed_out = (
        gated * lax.rsqrt(gated_stat / inner_width + EPS)[..., None] * gated_norm_gain
    ).astype(jnp.bfloat16)
    mamba_part = tp_total(
        row_gather(normed_out.reshape(local_rows, inner_local), mamba_output_weight)
    )
    layer_out = (block_out + mamba_part).astype(jnp.bfloat16).reshape(requests, new_tok, columns)
    return (layer_out, updated_state)


def solution(mesh):
    in_specs = (
        P(None, None, "seq"),
        P(None, None, "seq"),
        P(),
        P(),
        P(None, "seq", "tp"),
        P(None, "seq", "tp"),
        P(None, "seq"),
        P(None, None, "seq", "tp"),
        P("tp", "seq"),
        P("seq"),
        P(None, "seq", "tp"),
        P("seq", None),
        P(None, None, "tp"),
        P("tp", "seq"),
        P("seq"),
        P(None, "seq", "tp"),
        P("seq", "tp"),
        P("seq", None),
        P(None, "tp"),
        P(),
        P("seq", None, "tp"),
        P("seq", None, None),
        P("tp"),
        P("tp"),
        P("tp"),
        P("seq", "tp", None, None),
        P("tp"),
        P("tp", "seq"),
    )
    out_specs = (P(None, None, "seq"), P("seq", "tp", None, None))
    return jax.shard_map(
        on_device, mesh=mesh, in_specs=in_specs, out_specs=out_specs, check_vma=False
    )
```

profile of v0, /device:TPU:0, one launch (start us, length us, event | category | flops | bytes accessed | tf_op | source)
XLA Modules:
  0.0 990.6 jit_solution(5866142394799759688)
XLA Ops:
  8.4 68.4 %psum.98 = f32[128]{0:T(128)S(1)} all-reduce(f32[128]{0:T(128)S(1)} %add.258), channel_id=1, replica_groups=mesh['seq'=32,'tp'=4] {'seq'}, use_global_device_ids=true, to_apply=%region_2.0 | all-reduce | flops 128 | bytes 1024 | tf_op jit(solution)/shard_map/psum | solution.py:18
  82.6 140.1 %all-reduce.15 = (bf16[128,1024]{1,0:T(8,128)(2,1)S(1)}, bf16[128,1024]{1,0:T(8,128)(2,1)S(1)}, bf16[128,1024]{1,0:T(8,128)(2,1)S(1)}) all-reduce(f32[128,1024]{1,0:T(8,128)S(1)} %convolution_add_fusion.4, f32[128,1024]{1,0:T(8,128)S(1)} %convolution_add_fusion.3, ...), channel_id=1, replica_groups=mesh['seq'=32,'tp'=4] {'seq'}, use_global_device_ids=true, to_apply=%region_3.0 | all-reduce | flops 393216 | bytes 2359296 | tf_op jit(solution)/shard_map/psum | solution.py:18
  224.3 13.7 %while.18 = (s32[]{:T(128)}, f32[128,8]{0,1:T(8,128)S(1)}, f32[128,8]{0,1:T(8,128)S(1)}, f32[128,8,128]{0,2,1:T(8,128)S(1)}, s32[]{:T(128)}, /*index=5*/s32[128]...) while((s32[]{:T(128)}, f32[128,8]{0,1:T(8,128)S(1)}, ...), condition=%wide.region_12.13_spmd.clone, body=%wide.region_9.12_spmd.clone.sunk | while | flops 472221952 | bytes 9904335 | solution.py:185
  238.1 62.8 %pmax.7 = f32[128,8]{0,1:T(8,128)S(1)} all-reduce(f32[128,8]{0,1:T(8,128)S(1)} %get-tuple-element.189), channel_id=1, replica_groups=mesh['seq'=32,'tp'=4] {'seq'}, use_global_device_ids=true, to_apply=%region_13.14 | all-reduce | flops 1024 | bytes 8192 | tf_op jit(solution)/shard_map/pmax | solution.py:188
  301.9 62.7 %psum.103 = f32[128,8]{0,1:T(8,128)S(1)} all-reduce(f32[128,8]{0,1:T(8,128)S(1)} %get-tuple-element.301), channel_id=1, replica_groups=mesh['seq'=32,'tp'=4] {'seq'}, use_global_device_ids=true, to_apply=%region_15.16 | all-reduce | flops 1024 | bytes 8192 | tf_op jit(solution)/shard_map/psum | solution.py:18
  364.6 38.3 %all-reduce.10.cloned.1.call-done = f32[128,8,128]{0,2,1:T(8,128)} async-done(((f32[128,8,128]{0,2,1:T(8,128)}), f32[128,8,128]{0,2,1:T(8,128)}) %all-reduce.10.cloned.1.call-update) | async-done | bytes 524304 | tf_op jit(solution)/shard_map/psum | solution.py:18
  404.2 17.1 %psum.104 = f32[128,64]{0,1:T(8,128)S(1)} all-reduce(f32[128,64]{0,1:T(8,128)S(1)} %fusion.107), channel_id=1, replica_groups=mesh['seq'=32,'tp'=4] {'tp'}, use_global_device_ids=true, to_apply=%region_16.17 | all-reduce | flops 8192 | bytes 65536 | tf_op jit(solution)/shard_map/psum | solution.py:22
  421.2 62.7 %psum.105 = f32[128]{0:T(128)S(1)} all-reduce(f32[128]{0:T(128)S(1)} %get-tuple-element.299), channel_id=1, replica_groups=mesh['seq'=32,'tp'=4] {'seq'}, use_global_device_ids=true, to_apply=%region_18.19 | all-reduce | flops 128 | bytes 1024 | tf_op jit(solution)/shard_map/psum | solution.py:18
  484.7 1.4 pad_maximum_fusion
  488.1 1.5 fusion.101
  489.8 124.0 %psum.107 = bf16[128,128]{1,0:T(8,128)(2,1)S(1)} all-reduce(f32[128,128]{1,0:T(8,128)S(1)} %fusion.103), channel_id=1, replica_groups=mesh['seq'=32,'tp'=4] {'seq'}, use_global_device_ids=true, to_apply=%region_20.21 | all-reduce | flops 16384 | bytes 98304 | tf_op jit(solution)/shard_map/psum | solution.py:18
  613.9 1.7 convolution_add_fusion.1
  615.6 2.0 fusion.15
  617.7 14.4 %psum.108 = f32[128,64]{0,1:T(8,128)S(1)} all-reduce(f32[128,64]{0,1:T(8,128)S(1)} %fusion.15), channel_id=1, replica_groups=mesh['seq'=32,'tp'=4] {'tp'}, use_global_device_ids=true, to_apply=%region_21.22 | all-reduce | flops 8192 | bytes 65536 | tf_op jit(solution)/shard_map/psum | solution.py:22
  632.1 62.7 %psum.109 = f32[128]{0:T(128)S(1)} all-reduce(f32[128]{0:T(128)S(1)} %get-tuple-element.297), channel_id=1, replica_groups=mesh['seq'=32,'tp'=4] {'seq'}, use_global_device_ids=true, to_apply=%region_23.24 | all-reduce | flops 128 | bytes 1024 | tf_op jit(solution)/shard_map/psum | solution.py:18
  696.4 124.0 %all-reduce = f32[128,16]{1,0:T(8,128)S(1)} all-reduce(f32[128,16]{1,0:T(8,128)S(1)} %fusion.104), channel_id=2, replica_groups=mesh['seq'=32,'tp'=4] {'seq'}, use_global_device_ids=true, to_apply=%region_24.25.clone | all-reduce | flops 2048 | bytes 16384
  821.6 100.6 %all-reduce.14.cloned.1.call-done = (f32[128,128]{1,0:T(8,128)}, f32[128,2,1024]{2,0,1:T(8,128)}) async-done(((f32[128,128]{1,0:T(8,128)}, f32[128,2,1024]{2,0,1:T(8,128)}), (f32[128,128]{1,0:T(8,128)}, f32[128,2,1024]{2,0,1:T(8,128)})) %all-reduce.14.cloned.1.call-update) | async-done | bytes 1114128
  925.2 1.4 fusion.28
  926.6 1.5 fusion.26
  928.1 1.7 fusion.24
  930.6 1.3 fusion.22
  932.8 10.5 %psum.110 = f32[1,4]{1,0:T(1,128)S(1)} all-reduce(f32[1,4]{1,0:T(1,128)S(1)} %bitcast.284), channel_id=1, replica_groups=mesh['seq'=32,'tp'=4] {'tp'}, use_global_device_ids=true, to_apply=%region_28.29 | all-reduce | flops 4 | bytes 32 | tf_op jit(solution)/shard_map/psum | solution.py:22
  943.3 25.3 %all-gather = bf16[32,4,1024]{2,1,0:T(4,128)(2,1)S(1)} all-gather(bf16[1,4,1024]{2,1,0:T(4,128)(2,1)S(1)} %fusion.88), channel_id=1, replica_groups=mesh['seq'=32,'tp'=4] {'seq'}, dimensions={0}, use_global_device_ids=true | all-gather | bytes 270336 | tf_op jit(solution)/shard_map/all_gather | solution.py:35
  968.9 14.4 %psum.111 = f32[128,64]{0,1:T(8,128)S(1)} all-reduce(f32[128,64]{0,1:T(8,128)S(1)} %fusion.106), channel_id=1, replica_groups=mesh['seq'=32,'tp'=4] {'tp'}, use_global_device_ids=true, to_apply=%region_29.30 | all-reduce | flops 8192 | bytes 65536 | tf_op jit(solution)/shard_map/psum | solution.py:22
  (196 shorter events, 34.7 us)
Async XLA Ops:
  7.2 608.4 %copy-start = (bf16[2048,64]{0,1:T(8,128)(2,1)S(1)}, bf16[2048,64]{0,1:T(8,128)(2,1)}, u32[]{:S(2)}) copy-start(bf16[2048,64]{0,1:T(8,128)(2,1)} %param.43) | copy-start | bytes 786436
  7.2 74.8 %copy-start.4 = (bf16[3,2,64,1024]{3,2,1,0:T(8,128)(2,1)S(1)}, bf16[3,2,64,1024]{3,2,1,0:T(8,128)(2,1)}, u32[]{:S(2)}) copy-start(bf16[3,2,64,1024]{3,2,1,0:T(8,128)(2,1)} %param.37) | copy-start | bytes 2359300
  7.2 395.7 %all-reduce.10.cloned.1.call-start = ((), (), s32[]{:S(2)}) async-start(), calls=%async_computation | async-start | bytes 1048576 | tf_op jit(solution)/shard_map/psum | solution.py:18
  222.7 1.6 copy-start.24
  224.3 77.5 %copy-start.6 = (bf16[32,4,64]{2,1,0:T(4,128)(2,1)S(1)}, bf16[32,4,64]{2,1,0:T(4,128)(2,1)}, u32[]{:S(2)}) copy-start(bf16[32,4,64]{2,1,0:T(4,128)(2,1)} %param.30) | copy-start | bytes 49156
  238.0 165.9 %copy-start.8 = (bf16[1024,64]{0,1:T(8,128)(2,1)S(1)}, bf16[1024,64]{0,1:T(8,128)(2,1)}, u32[]{:S(2)}) copy-start(bf16[1024,64]{0,1:T(8,128)(2,1)} %param.38) | copy-start | bytes 393220
  238.0 245.9 %copy-start.18 = (f32[64]{0:T(128)S(1)}, f32[64]{0:T(128)}, u32[]{:S(2)}) copy-start(f32[64]{0:T(128)} %param.39) | copy-start | bytes 772
  238.0 246.0 %copy-start.5 = (bf16[2,64,2048]{2,1,0:T(8,128)(2,1)S(1)}, bf16[2,64,2048]{2,1,0:T(8,128)(2,1)}, u32[]{:S(2)}) copy-start(bf16[2,64,2048]{2,1,0:T(8,128)(2,1)} %param.40) | copy-start | bytes 1572868
  301.8 312.1 %all-reduce.12.cloned.1.call-start = ((), (), s32[]{:S(2)}) async-start(), calls=%async_computation.1 | async-start | bytes 4194304 | tf_op jit(solution)/shard_map/psum | solution.py:18
  486.1 2.0 copy-start.10
  486.1 2.0 copy-start.1
  486.2 436.0 %all-reduce.14.cloned.1.call-start = ((), (), s32[]{:S(2)}) async-start(), calls=%async_computation.2 | async-start | bytes 2228224
  488.1 1.5 copy-start.11
  615.6 79.2 %copy-start.19 = (f32[64]{0:T(128)S(1)}, f32[64]{0:T(128)}, u32[]{:S(2)}) copy-start(f32[64]{0:T(128)} %param.44) | copy-start | bytes 772
  615.6 79.3 %copy-start.7 = (bf16[2,64,1024]{2,1,0:T(8,128)(2,1)S(1)}, bf16[2,64,1024]{2,1,0:T(8,128)(2,1)}, u32[]{:S(2)}) copy-start(bf16[2,64,1024]{2,1,0:T(8,128)(2,1)} %param.45) | copy-start | bytes 786436
  615.6 79.8 %copy-start.12 = (bf16[64,128]{1,0:T(8,128)(2,1)S(1)}, bf16[64,128]{1,0:T(8,128)(2,1)}, u32[]{:S(2)}) copy-start(bf16[64,128]{1,0:T(8,128)(2,1)} %param.47) | copy-start | bytes 49156
  615.6 80.6 %copy-start.15 = (bf16[64,16]{0,1:T(8,128)(2,1)S(1)}, bf16[64,16]{0,1:T(8,128)(2,1)}, u32[]{:S(2)}) copy-start(bf16[64,16]{0,1:T(8,128)(2,1)} %param.46) | copy-start | bytes 6148
  695.1 126.4 %copy-start.22 = (f32[16]{0:T(128)S(1)}, f32[16]{0:T(128)}, u32[]{:S(2)}) copy-start(f32[16]{0:T(128)} %param.53) | copy-start | bytes 196
  695.2 126.4 %copy-start.23 = (f32[16]{0:T(128)S(1)}, f32[16]{0:T(128)}, u32[]{:S(2)}) copy-start(f32[16]{0:T(128)} %param.52) | copy-start | bytes 196
  695.4 229.7 %copy-start.2 = (f32[1,16,64,64]{3,2,1,0:T(8,128)S(1)}, f32[1,16,64,64]{3,2,1,0:T(8,128)}, u32[]{:S(2)}) copy-start(f32[1,16,64,64]{3,2,1,0:T(8,128)} %param.55) | copy-start | bytes 786436
  926.6 5.3 copy-start.20
  926.6 16.7 %copy-start.14 = (f32[1024]{0:T(1024)S(1)}, f32[1024]{0:T(1024)}, u32[]{:S(2)}) copy-start(f32[1024]{0:T(1024)} %param.56) | copy-start | bytes 12292
  928.1 40.6 %copy-start.9 = (bf16[1024,64]{0,1:T(8,128)(2,1)S(1)}, bf16[1024,64]{0,1:T(8,128)(2,1)}, u32[]{:S(2)}) copy-start(bf16[1024,64]{0,1:T(8,128)(2,1)} %param.57) | copy-start | bytes 393220
  930.5 53.5 %copy-start.3 = (f32[1,16,64,64]{3,2,1,0:T(8,128)}, f32[1,16,64,64]{3,2,1,0:T(8,128)S(1)}, u32[]{:S(2)}) copy-start(f32[1,16,64,64]{3,2,1,0:T(8,128)S(1)} %multiply_add_fusion.1) | copy-start | bytes 786436
  (5 other events, 4.2 us)
Sparse Core Ops, SparseCore 0:
  301.9 100.9 all-reduce.9
  486.3 102.3 all-reduce.11
  821.7 100.5 all-reduce.13
where the time goes:
time: 991 us
  blocking collectives  789 us (80%)
  waiting for transfers between devices  139 us (14%)
  matrix products  22.6 us (2%)
  between operations  15 us (2%)
  local copies, waits for them, and re-layouts  14 us (1%)
  other arithmetic  10.5 us (1%)
    psum x6, blocking collectives, sequence_total(): return lax.psum(values, 'seq')  521 us
    unnamed x1, blocking collectives  124 us
    unnamed x4, waiting for transfers between devices  101 us
    pmax x1, blocking collectives, on_device(): top_score = lax.pmax(maxima, 'seq')  62.8 us
    psum x4, blocking collectives, tp_total(): return lax.psum(values, 'tp')  56.4 us
    psum x2, waiting for transfers between devices, sequence_total(): return lax.psum(values, 'seq')  38.3 us
    all_gather x1, blocking collectives, row_gather(): lax.all_gather(rows_part, 'seq', axis=0, tiled=True)  25.3 us
  transfers between devices with their start and end apart: 3, of which 2 were waited for; matrix products, arithmetic and copies ran while one was open for 0% of the time, Pallas kernels for 0%

commit v1 on v0

v1 whole, which is shorter than its diff:
```python
import functools
import math

import jax
import jax.numpy as jnp
from jax import lax
from jax.experimental import pallas as pl
from jax.experimental.pallas import tpu as pltpu
from jax.sharding import PartitionSpec as P


HD = 128
MAMBA_HEAD_SIZE = 64
EPS = 1e-05
HIGHEST = lax.Precision.HIGHEST
NEG_FILL = -1e30
BF16 = jnp.bfloat16
F32 = jnp.float32


def core_swap(values):
    size = lax.axis_size("seq")
    return lax.ppermute(values, "seq", [(i, i ^ 1) for i in range(size)])


def project_kernel(weights_count, stat_lane, *refs):
    rows_ref, gain_ref = refs[:2]
    weight_refs = refs[2 : 2 + 2 * weights_count]
    out_ref = refs[-1]
    part = rows_ref[...]
    scaled = (part * gain_ref[...]).astype(BF16)
    at = 0
    for own_ref, partner_ref in zip(weight_refs[:weights_count], weight_refs[weights_count:]):
        stacked = len(own_ref.shape) == 3
        for which in range(own_ref.shape[0] if stacked else 1):
            own = own_ref[which] if stacked else own_ref[...]
            partner = partner_ref[which] if stacked else partner_ref[...]
            lanes = slice(at, at + own.shape[1])
            product = jnp.dot(
                scaled, jnp.concatenate([own, partner], axis=0), preferred_element_type=F32
            )
            at = lanes.stop
            if at < out_ref.shape[1]:
                out_ref[:, lanes] = product.astype(BF16)
    if at < out_ref.shape[1]:
        product = jnp.zeros((part.shape[0], HD), F32)
    total = jnp.sum(part * part, axis=1, keepdims=True)
    high = total.astype(BF16).astype(F32)
    lane = lax.broadcasted_iota(jnp.int32, product.shape, 1)
    product = jnp.where(lane == stat_lane, high, product)
    product = jnp.where(lane == stat_lane + 1, total - high, product)
    out_ref[:, out_ref.shape[1] - HD :] = product.astype(BF16)


def on_chip(values):
    return pltpu.with_memory_space_constraint(values, pltpu.VMEM)


def project(rows, gain, own_weights, partner_weights, stat_lane=0):
    columns = sum(math.prod(weight.shape) // weight.shape[-2] for weight in own_weights)
    columns = columns if stat_lane else columns + HD
    operands = [rows, gain] + list(own_weights) + list(partner_weights)
    return pl.pallas_call(
        functools.partial(project_kernel, len(own_weights), stat_lane),
        in_specs=[pl.BlockSpec(memory_space=pltpu.VMEM)] * len(operands),
        out_specs=pl.BlockSpec(memory_space=pltpu.VMEM),
        out_shape=pltpu.VMEM((rows.shape[0], columns), BF16),
        name="project",
    )(*[on_chip(operand) for operand in operands])


def entry_kernel(
    hidden_hbm,
    embedded_hbm,
    gain_hbm,
    weight_hbm,
    factor_ref,
    mine_out,
    other_out,
    hidden_mine_out,
    hidden_other_out,
    hidden_ref,
    embedded_ref,
    gain_ref,
    weight_ref,
    row_sem,
    gain_sem,
    weight_sem,
):
    core = lax.rem(lax.axis_index("seq"), 2)
    row_copies = []
    for side, parity in enumerate((core, 1 - core)):
        row_copies.append(
            pltpu.make_async_copy(
                hidden_hbm.at[:, parity], hidden_ref.at[side], row_sem.at[0, side]
            )
        )
        row_copies.append(
            pltpu.make_async_copy(
                embedded_hbm.at[:, parity], embedded_ref.at[side], row_sem.at[1, side]
            )
        )
    gain_copy = pltpu.make_async_copy(gain_hbm, gain_ref, gain_sem)
    count, _, columns = weight_ref.shape
    weight_copies = [
        pltpu.make_async_copy(weight_hbm.at[which], weight_ref.at[which], weight_sem.at[which])
        for which in range(count)
    ]
    for copy in row_copies + [gain_copy] + weight_copies:
        copy.start()
    for copy in row_copies + [gain_copy]:
        copy.wait()
    requests = hidden_ref.shape[1]

    def joined(side):
        return jnp.concatenate(
            [
                jnp.concatenate(
                    [ref[side, request].astype(F32) for request in range(requests)], axis=0
                )
                for ref in (hidden_ref, embedded_ref)
            ],
            axis=1,
        )

    gain = jnp.concatenate([gain_ref[0:1, :], gain_ref[1:2, :]], axis=1)
    parts = [joined(0), joined(1)]
    outs = [mine_out, other_out]
    width = count * columns
    half = parts[0].shape[1] // 2
    hidden_mine_out[...] = parts[0][:, :half]
    hidden_other_out[...] = parts[1][:, :half].astype(BF16)
    scaled = []
    for part, parity in zip(parts, (core, 1 - core)):
        factor = jnp.concatenate(
            [factor_ref[request, parity] for request in range(requests)], axis=0
        )
        scaled.append((part * factor * gain).astype(BF16))
    for which in range(count):
        lanes = slice(which * columns, (which + 1) * columns)
        weight_copies[which].wait()
        for side in (1, 0):
            product = jnp.dot(scaled[side], weight_ref[which], preferred_element_type=F32)
            narrow = product.astype(outs[side].dtype)
            outs[side][:, lanes] = narrow
            if which == 0 and side == 1:
                outs[side][:, width : width + columns] = (
                    product - narrow.astype(F32)
                ).astype(BF16)


def enter(hidden, embedded, gain, weight, factor):
    requests, new_tok, half = hidden.shape
    split = (requests // 2, 2, new_tok, half)
    rows = requests // 2 * new_tok
    count, _, columns = weight.shape
    width = count * columns
    vmem = pl.BlockSpec(memory_space=pltpu.VMEM)
    anywhere = pl.BlockSpec(memory_space=pl.ANY)
    side = (2, requests // 2, new_tok, half)
    return pl.pallas_call(
        entry_kernel,
        in_specs=[anywhere] * 4 + [vmem],
        out_specs=[vmem] * 4,
        out_shape=[
            pltpu.VMEM((rows, width), F32),
            pltpu.VMEM((rows, width + columns), BF16),
            pltpu.VMEM((rows, half), F32),
            pltpu.VMEM((rows, half), BF16),
        ],
        scratch_shapes=[
            pltpu.VMEM(side, BF16),
            pltpu.VMEM(side, BF16),
            pltpu.VMEM(gain.shape, F32),
            pltpu.VMEM(weight.shape, BF16),
            pltpu.SemaphoreType.DMA((2, 2)),
            pltpu.SemaphoreType.DMA,
            pltpu.SemaphoreType.DMA((count,)),
        ],
        name="enter",
    )(
        hidden.reshape(split),
        embedded.reshape(split),
        gain,
        weight,
        on_chip(factor.reshape(split[:3] + (factor.shape[-1],))),
    )


def merge_kernel(query_columns, mine_ref, received_ref, out_ref):
    width = mine_ref.shape[1]
    query = slice(0, query_columns)
    low = slice(width, width + query_columns)
    total = (
        mine_ref[:, query]
        + received_ref[:, query].astype(F32)
        + received_ref[:, low].astype(F32)
    )
    high = total.astype(BF16)
    out_ref[:, query] = high
    out_ref[:, low] = (total - high.astype(F32)).astype(BF16)
    others = slice(query_columns, width)
    out_ref[:, others] = (
        mine_ref[:, others] + received_ref[:, others].astype(F32)
    ).astype(BF16)


def merge(mine, received, query_columns):
    return pl.pallas_call(
        functools.partial(merge_kernel, query_columns),
        in_specs=[pl.BlockSpec(memory_space=pltpu.VMEM)] * 2,
        out_specs=pl.BlockSpec(memory_space=pltpu.VMEM),
        out_shape=pltpu.VMEM(received.shape, BF16),
        name="merge",
    )(on_chip(mine), on_chip(received))


def spread_rows(part, new_tok):
    size = lax.axis_size("seq")
    part = part.reshape(size // 2, new_tok, part.shape[1])
    groups = [list(range(core, size, 2)) for core in range(2)]
    return lax.all_to_all(part, "seq", 0, 0, axis_index_groups=groups, tiled=True)


def summed_rows(spread_ref, lanes):
    total = spread_ref[0, :, lanes].astype(F32)
    for source in range(1, spread_ref.shape[0]):
        total = total + spread_ref[source, :, lanes].astype(F32)
    return total


def norm_factor(spread_ref, width, last):
    addends = summed_rows(spread_ref, slice(last - HD, last))
    return lax.rsqrt((addends[:, 0:1] + addends[:, 1:2]) / width + EPS)


def finish_kernel(query_columns, spread_ref, out_ref):
    end = out_ref.shape[1]
    query = summed_rows(spread_ref, slice(0, query_columns)) + summed_rows(
        spread_ref, slice(end, end + query_columns)
    )
    out_ref[:, :query_columns] = query.astype(BF16)
    rest = slice(query_columns, end)
    out_ref[:, rest] = summed_rows(spread_ref, rest).astype(BF16)


def finish_projection(spread, query_columns):
    _, new_tok, columns = spread.shape
    return pl.pallas_call(
        functools.partial(finish_kernel, query_columns),
        in_specs=[pl.BlockSpec(memory_space=pltpu.VMEM)],
        out_specs=pl.BlockSpec(memory_space=pltpu.VMEM),
        out_shape=pltpu.VMEM((new_tok, columns - query_columns), BF16),
        name="finish_projection",
    )(on_chip(spread))


def activation_kernel(width, spread_ref, adapter_ref, out_ref):
    rank, units = adapter_ref.shape[1:]
    factor = norm_factor(spread_ref, width, spread_ref.shape[2])
    low_rank = summed_rows(spread_ref, slice(2 * units, 2 * units + rank)) * factor
    low_rank = low_rank.astype(BF16)

    def pre(which):
        direct = summed_rows(spread_ref, slice(which * units, (which + 1) * units))
        return direct * factor + jnp.dot(
            low_rank, adapter_ref[which], preferred_element_type=F32
        )

    out_ref[...] = (silu(pre(0)) * pre(1)).astype(BF16)


def activate(spread, adapter, width):
    return pl.pallas_call(
        functools.partial(activation_kernel, width),
        in_specs=[pl.BlockSpec(memory_space=pltpu.VMEM)] * 2,
        out_specs=pl.BlockSpec(memory_space=pltpu.VMEM),
        out_shape=pltpu.VMEM((spread.shape[1], adapter.shape[2]), BF16),
        name="activate",
    )(on_chip(spread), on_chip(adapter))


def gather_rows(block):
    size = lax.axis_size("seq")
    full = jnp.broadcast_to(block[None], (size,) + block.shape)
    return lax.all_to_all(full, "seq", 0, 0, tiled=True)


def gather_core_rows(block):
    size = lax.axis_size("seq")
    new_tok, columns = block.shape
    full = jnp.broadcast_to(block[None], (size // 2,) + block.shape)
    groups = [list(range(core, size, 2)) for core in range(2)]
    rows = lax.all_to_all(full, "seq", 0, 0, axis_index_groups=groups, tiled=True)
    return rows.reshape(size // 2 * new_tok, columns)


TP_STEPS = (2, 1, 3)


def swap_all(arrays):
    swapped = []
    for array in arrays:
        swapped.append(core_swap(array))
    return swapped


def tp_total(values, beside=None):
    size = lax.axis_size("tp")
    narrow = values.astype(BF16)
    parts = []
    for step in TP_STEPS:
        pairs = [(i, (i + step) % size) for i in range(size)]
        parts.append(lax.ppermute(narrow, "tp", pairs))
    parts, beside = lax.optimization_barrier((parts, beside))
    total = values
    for part in parts:
        total = total + part.astype(F32)
    return total, beside


def attention_kernel(
    group_ref, limit_ref, query_ref, key_hbm, value_hbm, out_ref, key_ref, value_ref, key_sem, value_sem
):
    rows, width = query_ref.shape
    groups, cache_len, _ = key_hbm.shape
    heads = width // HD
    pairs = heads // 2

    def key_copy(pair):
        lanes = pl.ds(pair * 2 * HD, 2 * HD)
        return pltpu.make_async_copy(
            key_hbm.at[:, :, lanes], key_ref.at[pair], key_sem.at[pair]
        )

    def value_copy(pair):
        lanes = pl.ds(pair * 2 * HD, 2 * HD)
        return pltpu.make_async_copy(
            value_hbm.at[:, :, lanes], value_ref.at[pair], value_sem.at[pair]
        )

    for pair in range(pairs):
        key_copy(pair).start()
        value_copy(pair).start()
    group_of = jnp.concatenate([group_ref[...], group_ref[...]], axis=0)
    position = lax.broadcasted_iota(jnp.int32, (rows, cache_len), 1)
    seen = jnp.where(position < limit_ref[...], 1, 0)
    valid = jnp.concatenate([seen, seen], axis=0) > 0
    lane = lax.broadcasted_iota(jnp.int32, (rows, HD), 1)
    code = jnp.zeros((rows, HD), F32)
    blank = jnp.zeros((rows, HD), BF16)

    def scores_of(pair):
        at = pair * 2 * HD
        first = jnp.concatenate([query_ref[:, at : at + HD], blank], axis=1)
        second = jnp.concatenate([blank, query_ref[:, at + HD : at + 2 * HD]], axis=1)
        query = jnp.concatenate([first, second], axis=0)
        scores = jnp.full((2 * rows, cache_len), NEG_FILL, F32)
        for group in range(groups):
            group_scores = lax.dot_general(
                query,
                key_ref[pair, group],
                (((1,), (1,)), ((), ())),
                preferred_element_type=F32,
            )
            scores = jnp.where(group_of == group, group_scores, scores)
        return jnp.where(valid, scores * (1.0 / math.sqrt(HD)), NEG_FILL)

    def finish(pair, scores, code):
        top = jnp.max(scores, axis=1, keepdims=True)
        weights = jnp.where(valid, jnp.exp(scores - top), 0.0)
        total = jnp.sum(weights, axis=1, keepdims=True)
        wide = jnp.concatenate(
            [
                jnp.where(group_of == group, weights, 0.0).astype(BF16)
                for group in range(groups)
            ],
            axis=1,
        )
        values = value_ref[pair].reshape(groups * cache_len, 2 * HD)
        summed = jnp.dot(wide, values, preferred_element_type=F32)
        safe = jnp.maximum(total, 1e-30)
        scaled = (summed / safe).astype(BF16)
        lse = jnp.where(total > 0.0, top + jnp.log(safe), NEG_FILL)
        high = lse.astype(BF16).astype(F32)
        mid = (lse - high).astype(BF16).astype(F32)
        low = lse - high - mid
        for here in range(2):
            head = 2 * pair + here
            part = slice(here * rows, (here + 1) * rows)
            out_ref[:, head * HD : (head + 1) * HD] = scaled[
                part, here * HD : (here + 1) * HD
            ]
            code = jnp.where(lane == head, high[part], code)
            code = jnp.where(lane == head + heads, mid[part], code)
            code = jnp.where(lane == head + 2 * heads, low[part], code)
        return code

    before = None
    for pair in range(pairs):
        key_copy(pair).wait()
        if pair:
            value_copy(pair - 1).wait()
        scores = scores_of(pair)
        if pair:
            code = finish(pair - 1, before, code)
        before = scores
    value_copy(pairs - 1).wait()
    code = finish(pairs - 1, before, code)
    out_ref[:, width:] = code.astype(BF16)


def attention_partials(query, key_cache, value_cache, group_of, limit):
    rows, width = query.shape
    groups, cache_len, _ = key_cache.shape
    pairs = width // (2 * HD)
    vmem = pl.BlockSpec(memory_space=pltpu.VMEM)
    anywhere = pl.BlockSpec(memory_space=pl.ANY)
    return pl.pallas_call(
        attention_kernel,
        in_specs=[vmem, vmem, vmem, anywhere, anywhere],
        out_specs=vmem,
        out_shape=pltpu.VMEM((rows, width + HD), BF16),
        scratch_shapes=[
            pltpu.VMEM((pairs, groups, cache_len, 2 * HD), BF16),
            pltpu.VMEM((pairs, groups, cache_len, 2 * HD), BF16),
            pltpu.SemaphoreType.DMA((pairs,)),
            pltpu.SemaphoreType.DMA((pairs,)),
        ],
        name="cache_attention",
    )(on_chip(group_of), on_chip(limit), on_chip(query), key_cache, value_cache)


def combine_kernel(spread_ref, own_ref, out_ref):
    new_tok, width = out_ref.shape
    heads = width // HD
    code = spread_ref[:, :, width:].astype(F32)
    peers = code + pltpu.roll(code, HD - heads, 2) + pltpu.roll(code, HD - 2 * heads, 2)
    own = own_ref[...].astype(F32)
    query, keys, values = own[:, :width], own[:, width : 2 * width], own[:, 2 * width :]
    products = jnp.concatenate(
        [query * keys[source : source + 1] for source in range(new_tok)], axis=0
    )
    head_of = lax.broadcasted_iota(jnp.int32, (width, HD), 0) // HD
    collect = jnp.where(
        head_of == lax.broadcasted_iota(jnp.int32, (width, HD), 1), 1.0, 0.0
    ).astype(F32)
    scores = jnp.dot(
        products, collect, precision=HIGHEST, preferred_element_type=F32
    ) * (1.0 / math.sqrt(HD))
    token = lax.broadcasted_iota(jnp.int32, (new_tok, HD), 0)
    own_scores = [
        jnp.where(token >= source, scores[source * new_tok : (source + 1) * new_tok], NEG_FILL)
        for source in range(new_tok)
    ]
    top = jnp.max(peers, axis=0)
    for source in range(new_tok):
        top = jnp.maximum(top, own_scores[source])
    peer_weight = jnp.exp(peers - top[None])
    own_weight = [jnp.exp(own_score - top) for own_score in own_scores]
    total = jnp.sum(peer_weight, axis=0)
    for weight in own_weight:
        total = total + weight
    scale = 1.0 / total
    peer_weight = peer_weight * scale[None]
    own_weight = [weight * scale for weight in own_weight]
    for head in range(heads):
        lanes = slice(head * HD, (head + 1) * HD)
        summed = jnp.sum(
            peer_weight[:, :, head : head + 1] * spread_ref[:, :, lanes].astype(F32), axis=0
        )
        for source in range(new_tok):
            summed = (
                summed
                + own_weight[source][:, head : head + 1] * values[source : source + 1, lanes]
            )
        out_ref[:, lanes] = summed.astype(BF16)


def combine_partials(spread, own):
    _, new_tok, columns = spread.shape
    return pl.pallas_call(
        combine_kernel,
        in_specs=[pl.BlockSpec(memory_space=pltpu.VMEM)] * 2,
        out_specs=pl.BlockSpec(memory_space=pltpu.VMEM),
        out_shape=pltpu.VMEM((new_tok, columns - HD), BF16),
        name="combine",
    )(on_chip(spread), on_chip(own))


def chip_product_kernel(rows_ref, own_ref, partner_ref, out_ref):
    depth = own_ref.shape[1]
    weight = jnp.concatenate([own_ref[...], partner_ref[...]], axis=0)
    out_ref[...] = lax.dot_general(
        rows_ref[:, :depth],
        weight,
        (((1,), (1,)), ((), ())),
        preferred_element_type=F32,
    )


def chip_product(rows, own_weight, partner_weight):
    columns = 2 * own_weight.shape[1]
    return pl.pallas_call(
        chip_product_kernel,
        in_specs=[pl.BlockSpec(memory_space=pltpu.VMEM)] * 3,
        out_specs=pl.BlockSpec(memory_space=pltpu.VMEM),
        out_shape=pltpu.VMEM((rows.shape[0], columns), F32),
        name="chip_product",
    )(on_chip(rows), on_chip(own_weight.T), on_chip(partner_weight.T))


def silu(values):
    return values / (1.0 + jnp.exp(-values))


def mamba_kernel(
    width,
    spread_ref,
    tail_x_ref,
    tail_bc_ref,
    taps_x_ref,
    taps_bc_ref,
    bias_ref,
    rate_ref,
    skip_ref,
    state_ref,
    gain_ref,
    block_ref,
    update_ref,
    b_ref,
    carried_ref,
):
    sources, new_tok, _ = spread_ref.shape
    inner = tail_x_ref.shape[1]
    heads = bias_ref.shape[1]
    state_dim = state_ref.shape[1]
    bc_width = tail_bc_ref.shape[1]
    taps = taps_x_ref.shape[0]
    own = spread_ref[0].astype(F32)
    for source in range(1, sources):
        own = own + spread_ref[source].astype(F32)
    extra = own[:, 2 * inner + bc_width :]
    stat = extra[:, heads : heads + 1] + extra[:, heads + 1 : heads + 2]
    factor = lax.rsqrt(stat / width + EPS)
    own = own * factor
    dt_raw = own[:, 2 * inner + bc_width :][:, :heads]

    def conv(tail_ref, fresh, taps_ref):
        history = tail_ref[...].astype(F32)
        sequence = [history[t : t + 1] for t in range(taps - 1)]
        sequence = sequence + [fresh[t : t + 1] for t in range(new_tok)]
        mixed = []
        for token in range(new_tok):
            result = taps_ref[0:1, :] * sequence[token]
            for tap in range(1, taps):
                result = result + taps_ref[tap : tap + 1, :] * sequence[token + tap]
            mixed.append(silu(result))
        return mixed

    mixed_x = conv(tail_x_ref, own[:, inner : 2 * inner], taps_x_ref)
    mixed_bc = jnp.concatenate(
        conv(tail_bc_ref, own[:, 2 * inner : 2 * inner + bc_width], taps_bc_ref), axis=0
    )
    b_mat = mixed_bc[:, :state_dim]
    c_mat = pltpu.roll(mixed_bc, bc_width - state_dim, 1)[:, :state_dim]
    shifted = dt_raw + bias_ref[...]
    step = jnp.maximum(shifted, 0.0) + jnp.log1p(jnp.exp(-jnp.abs(shifted)))
    decay = jnp.exp(-step * rate_ref[...])
    steps = [step[t : t + 1] for t in range(new_tok)]
    decays = [decay[t : t + 1] for t in range(new_tok)]
    contract = (((1,), (1,)), ((), ()))
    mixing = lax.dot_general(
        c_mat, b_mat, contract, precision=HIGHEST, preferred_element_type=F32
    )
    from_state = lax.dot_general(
        c_mat, state_ref[...], contract, precision=HIGHEST, preferred_element_type=F32
    )
    carried = [decays[0]]
    for token in range(1, new_tok):
        carried.append(carried[-1] * decays[token])
    table = list(carried)
    place = {}
    last = new_tok - 1
    for source in range(new_tok):
        scaled = steps[source]
        for token in range(source, new_tok):
            if token > source:
                scaled = scaled * decays[token]
            weight = scaled * mixing[token : token + 1, source : source + 1]
            if token == source:
                weight = weight + skip_ref[...]
            place[token, source] = len(table)
            table.append(weight)
        place["update", source] = len(table)
        table.append(scaled)
    while len(table) % 8:
        table.append(jnp.zeros_like(table[0]))
    head_of = lax.broadcasted_iota(jnp.int32, (heads, inner), 1) // MAMBA_HEAD_SIZE
    expand = jnp.where(
        head_of == lax.broadcasted_iota(jnp.int32, (heads, inner), 0), 1.0, 0.0
    ).astype(F32)
    wide = jnp.dot(
        jnp.concatenate(table, axis=0), expand, precision=HIGHEST, preferred_element_type=F32
    )
    z_part = own[:, :inner]
    gain = gain_ref[...]
    lane = lax.broadcasted_iota(jnp.int32, (1, HD), 1)
    blocks, extras = [], []
    for token in range(new_tok):
        output = wide[token : token + 1] * from_state[token : token + 1]
        for source in range(token + 1):
            at = place[token, source]
            output = output + wide[at : at + 1] * mixed_x[source]
        gated = output * silu(z_part[token : token + 1])
        total = jnp.sum(gated * gated, axis=1, keepdims=True)
        high = total.astype(BF16).astype(F32)
        blocks.append(gated * gain)
        extras.append(
            jnp.where(lane == 0, high, jnp.where(lane == 1, total - high, 0.0))
        )
    block_ref[:, :inner] = jnp.concatenate(blocks, axis=0).astype(BF16)
    block_ref[:, inner:] = jnp.concatenate(extras, axis=0).astype(BF16)
    update_ref[...] = jnp.concatenate(
        [
            wide[place["update", source] : place["update", source] + 1] * mixed_x[source]
            for source in range(new_tok)
        ],
        axis=0,
    )
    b_ref[...] = b_mat
    carried_ref[...] = carried[last]


def mamba_step(
    spread, tail_x, tail_bc, taps_x, taps_bc, bias, rate, skip, state, gain, width
):
    new_tok = spread.shape[1]
    inner = tail_x.shape[1]
    heads = bias.shape[1]
    operands = (spread, tail_x, tail_bc, taps_x, taps_bc, bias, rate, skip, state, gain)
    return pl.pallas_call(
        functools.partial(mamba_kernel, width),
        in_specs=[pl.BlockSpec(memory_space=pltpu.VMEM)] * len(operands),
        out_specs=[pl.BlockSpec(memory_space=pltpu.VMEM)] * 4,
        out_shape=[
            pltpu.VMEM((new_tok, inner + HD), BF16),
            pltpu.VMEM((new_tok, inner), F32),
            pltpu.VMEM((new_tok, state.shape[1]), F32),
            pltpu.VMEM((1, heads), F32),
        ],
        name="mamba_step",
    )(*[on_chip(operand) for operand in operands])


def state_kernel(state_ref, update_ref, b_ref, carried_ref, out_ref):
    heads = carried_ref.shape[1]
    added = lax.dot_general(
        update_ref[...],
        b_ref[...],
        (((0,), (0,)), ((), ())),
        precision=HIGHEST,
        preferred_element_type=F32,
    )
    size = state_ref.shape[0] // heads
    for head in range(heads):
        part = slice(head * size, (head + 1) * size)
        out_ref[part] = carried_ref[0:1, head : head + 1] * state_ref[part] + added[part]


def state_update(state, update, b_mat, carried):
    return pl.pallas_call(
        state_kernel,
        in_specs=[pl.BlockSpec(memory_space=pltpu.VMEM)] * 4,
        out_specs=pl.BlockSpec(memory_space=pltpu.VMEM),
        out_shape=jax.ShapeDtypeStruct(state.shape, F32),
        name="state_update",
    )(*[on_chip(operand) for operand in (state, update, b_mat, carried)])


def on_device(
    hidden,
    embedded,
    request_group,
    group_prompt_length,
    prompt_key_cache,
    prompt_value_cache,
    input_norm_gain,
    query_key_value_weight,
    attention_output_weight,
    middle_norm_gain,
    gate_up_weight,
    adapter_down_weight,
    adapter_up_weight,
    down_weight,
    mamba_norm_gain,
    input_gate_x_weight,
    input_step_weight,
    input_bc_weight,
    convolution_x_taps,
    convolution_bc_taps,
    prompt_tail_x,
    prompt_tail_bc,
    step_bias,
    head_decay_rate,
    head_skip_gain,
    prompt_state,
    gated_norm_gain,
    mamba_output_weight,
):
    requests, new_tok, columns = hidden.shape
    rows = requests * new_tok
    seq_size = lax.axis_size("seq")
    width = columns * seq_size
    groups, cache_len, width_local = prompt_key_cache.shape
    row_group = jnp.repeat(request_group, new_tok)
    group_match = row_group[:, None] == jnp.arange(groups)[None, :]
    row_length = jnp.sum(jnp.where(group_match, group_prompt_length[None, :], 0), axis=1)
    start = lax.axis_index("seq") * cache_len
    plane = (rows, HD)
    group_of = jnp.broadcast_to(row_group[:, None], plane)
    limit = jnp.broadcast_to((row_length - start)[:, None], plane)

    stat = jnp.sum(jnp.square(hidden.astype(F32)), axis=-1) + jnp.sum(
        jnp.square(embedded.astype(F32)), axis=-1
    )
    stats = lax.all_to_all(
        jnp.broadcast_to(stat.reshape(1, 1, rows), (seq_size, 1, rows)),
        "seq",
        0,
        0,
        tiled=True,
    )
    early = swap_all(
        (
            gate_up_weight,
            attention_output_weight,
            adapter_down_weight,
            middle_norm_gain,
            mamba_norm_gain,
            down_weight,
        ),
    )
    middle_gain = jnp.concatenate([middle_norm_gain, early[3]])[None]
    mamba_gain = jnp.concatenate([mamba_norm_gain, early[4]])[None]
    stats, group_of, limit, middle_gain, mamba_gain = lax.optimization_barrier(
        (stats, group_of, limit, middle_gain, mamba_gain)
    )
    factor = lax.rsqrt(jnp.sum(stats, axis=(0, 1)) / (2 * width) + EPS)
    qkv_weight = query_key_value_weight.reshape(3, 2 * columns, width_local)
    from_mine, from_other, hidden_mine, hidden_other = enter(
        hidden,
        embedded,
        input_norm_gain,
        qkv_weight,
        jnp.broadcast_to(factor[:, None], (rows, 2 * columns)),
    )
    (
        received,
        hidden_partner,
        gate_up_partner,
        output_partner,
        adapter_down_partner,
        down_partner,
    ) = lax.optimization_barrier(
        (
            core_swap(from_other),
            core_swap(hidden_other),
            early[0],
            early[1],
            early[2],
            early[5],
        )
    )
    hidden_rows = jnp.concatenate([hidden_mine, hidden_partner.astype(F32)], axis=1)
    part, hidden_rows = lax.optimization_barrier(
        (merge(from_mine, received, width_local), hidden_rows)
    )
    spread = spread_rows(part, new_tok)
    own_qkv = finish_projection(spread, width_local)
    query = gather_rows(own_qkv[:, :width_local]).reshape(rows, width_local)
    pieces = attention_partials(query, prompt_key_cache, prompt_value_cache, group_of, limit)
    pieces = pieces.reshape(requests, new_tok, width_local + HD)
    own_attn = combine_partials(
        lax.all_to_all(pieces, "seq", 0, 0, tiled=True), own_qkv
    )
    attn = gather_core_rows(own_attn)
    summed, adapter_up = tp_total(
        chip_product(attn, attention_output_weight, output_partner),
        jnp.transpose(adapter_up_weight, (1, 0, 2)),
    )
    resid = hidden_rows + summed

    spread = spread_rows(
        project(
            resid,
            middle_gain,
            [gate_up_weight, adapter_down_weight],
            [gate_up_partner, adapter_down_partner],
        ),
        new_tok,
    )
    own_act = activate(spread, adapter_up, width)
    act = gather_core_rows(own_act)
    mamba_heads = input_step_weight.shape[1]
    step_pad = ((0, 0), (0, HD - mamba_heads))
    gate_x_partner, bc_partner, step_partner, mamba_output_partner = swap_all(
        (input_gate_x_weight, input_bc_weight, input_step_weight, mamba_output_weight),
    )
    beside = (
        jnp.pad(input_step_weight, step_pad),
        jnp.pad(step_partner, step_pad),
        gate_x_partner,
        bc_partner,
        mamba_output_partner,
    )
    summed, beside = tp_total(chip_product(act, down_weight, down_partner), beside)
    step_weight, step_partner, gate_x_partner, bc_partner, mamba_output_partner = beside
    block_out = resid + summed

    inner_local = input_gate_x_weight.shape[2]
    spread = spread_rows(
        project(
            block_out,
            mamba_gain,
            [input_gate_x_weight, input_bc_weight, step_weight],
            [gate_x_partner, bc_partner, step_partner],
            stat_lane=mamba_heads,
        ),
        new_tok,
    )
    state = prompt_state[0]
    block, update, b_mat, carried = mamba_step(
        spread,
        prompt_tail_x[0],
        prompt_tail_bc[0],
        convolution_x_taps,
        convolution_bc_taps,
        step_bias[None],
        head_decay_rate[None],
        head_skip_gain[None],
        state.reshape(inner_local, state.shape[-1]),
        gated_norm_gain[None],
        width,
    )
    normed = gather_core_rows(block)
    normed, update, b_mat, carried = lax.optimization_barrier(
        (normed, update, b_mat, carried)
    )
    updated_state = state_update(
        state.reshape(inner_local, state.shape[-1]), update, b_mat, carried
    ).reshape(prompt_state.shape)
    product = chip_product(normed, mamba_output_weight, mamba_output_partner)
    stat = (
        normed[:, inner_local : inner_local + 1].astype(F32)
        + normed[:, inner_local + 1 : inner_local + 2].astype(F32)
    )
    high = lax.reduce_precision(stat, 8, 7)
    addends = jnp.concatenate(
        [
            jnp.broadcast_to(high, (stat.shape[0], columns)),
            jnp.broadcast_to(stat - high, (stat.shape[0], columns)),
        ],
        axis=1,
    )
    both, updated_state = tp_total(
        jnp.concatenate([product, addends], axis=1), updated_state
    )
    gated_stat = both[:, 2 * columns : 3 * columns] + both[:, 3 * columns :]
    gated_stat = jnp.concatenate([gated_stat, gated_stat], axis=1)
    inner_width = inner_local * lax.axis_size("tp")
    factor = lax.rsqrt(gated_stat / inner_width + EPS)
    layer_out = (block_out + both[:, : 2 * columns] * factor).astype(BF16)
    mine = layer_out[:, :columns].reshape(requests // 2, new_tok, columns)
    other = core_swap(layer_out[:, columns:]).reshape(mine.shape)
    even_core = lax.axis_index("seq") % 2 == 0
    layer_out = jnp.stack(
        [jnp.where(even_core, mine, other), jnp.where(even_core, other, mine)], axis=1
    )
    return layer_out.reshape(requests, new_tok, columns), updated_state


def solution(mesh):
    in_specs = (
        P(None, None, "seq"),
        P(None, None, "seq"),
        P(),
        P(),
        P(None, "seq", "tp"),
        P(None, "seq", "tp"),
        P(None, "seq"),
        P(None, None, "seq", "tp"),
        P("tp", "seq"),
        P("seq"),
        P(None, "seq", "tp"),
        P("seq", None),
        P(None, None, "tp"),
        P("tp", "seq"),
        P("seq"),
        P(None, "seq", "tp"),
        P("seq", "tp"),
        P("seq", None),
        P(None, "tp"),
        P(),
        P("seq", None, "tp"),
        P("seq", None, None),
        P("tp"),
        P("tp"),
        P("tp"),
        P("seq", "tp", None, None),
        P("tp"),
        P("tp", "seq"),
    )
    out_specs = (P(None, None, "seq"), P("seq", "tp", None, None))
    return jax.shard_map(
        on_device, mesh=mesh, in_specs=in_specs, out_specs=out_specs, check_vma=False
    )
```

time: 991 us -> 164 us (0.17)
  blocking collectives: 789 us -> 88.3 us
  waiting for transfers between devices: 139 us -> 20.2 us
  starting transfers between devices: 0.12 us -> 29.8 us
  matrix products: 22.6 us -> 0 us
  between operations: 15 us -> 1.3 us
  Pallas kernels: 0 us -> 10.8 us
    psum x10 -> x0, blocking collectives: 577 us -> none  [the longest x6 521 us: sequence_total(): return lax.psum(values, 'seq')]
    unnamed x1 -> x0, blocking collectives: 124 us -> none
    unnamed x4 -> x0, waiting for transfers between devices: 101 us -> none
    all_to_all x0 -> x7, blocking collectives: none -> 88.3 us  [the longest x3 41.3 us: spread_rows(): lax.all_to_all(part, 'seq', 0, 0, axis_index_groups=groups, tiled=True)]
    pmax x1 -> x0, blocking collectives: 62.8 us -> none  [on_device(): top_score = lax.pmax(maxima, 'seq')]
    psum x2 -> x0, waiting for transfers between devices: 38.3 us -> none  [sequence_total(): return lax.psum(values, 'seq')]
    all_gather x1 -> x0, blocking collectives: 25.3 us -> none  [row_gather(): lax.all_gather(rows_part, 'seq', axis=0, tiled=True)]
    dot_general x31 -> x0, matrix products: 22.6 us -> none  [the longest x4 5.9 us: state_space_scan(): jnp.einsum('rhps,rs->rhp', state, c_mat[:, token_index], precision=HIGHEST)]
  transfers between devices with their start and end apart: 3 -> 24, of which waited for: 2 -> 11; matrix products, arithmetic and copies ran while one was open for 0% -> 3% of each run, Pallas kernels for 0% -> 2%
where the time goes in v1:
time: 164 us; the launch traced here: 162 us
  blocking collectives  88.3 us (54%)
  starting transfers between devices  29.8 us (18%)
  waiting for transfers between devices  20.2 us (12%)
  Pallas kernels  10.8 us (7%)
  local copies, waits for them, and re-layouts  7.03 us (4%)
  other arithmetic  4.59 us (3%)
    all_to_all x3, blocking collectives, spread_rows(): lax.all_to_all(part, 'seq', 0, 0, axis_index_groups=groups, tiled=True)  41.3 us
    all_to_all x2, blocking collectives, gather_core_rows(): lax.all_to_all(full, 'seq', 0, 0, axis_index_groups=groups, tiled=True)  22.2 us
    ppermute x9, starting transfers between devices, tp_total(): parts.append(lax.ppermute(narrow, 'tp', pairs))  14.4 us
    all_to_all x1, blocking collectives, on_device(): lax.all_to_all(pieces, 'seq', 0, 0, tiled=True)  12.9 us
    all_to_all x1, blocking collectives, gather_rows(): return lax.all_to_all(full, 'seq', 0, 0, tiled=True)  11.9 us
    all_to_all x1, starting transfers between devices, on_device(): lax.all_to_all(jnp.broadcast_to(stat.reshape(1, 1, rows), (seq_size, 1, r...  8.27 us
    all_to_all x1, waiting for transfers between devices, gather_core_rows(): lax.all_to_all(full, 'seq', 0, 0, axis_index_groups=groups, tiled=True)  7.18 us
    ppermute x9, waiting for transfers between devices, tp_total(): parts.append(lax.ppermute(narrow, 'tp', pairs))  5.93 us
  transfers between devices with their start and end apart: 24, of which 11 were waited for; matrix products, arithmetic and copies ran while one was open for 3% of the time, Pallas kernels for 2%

profile of v1, /device:TPU:0, one launch (start us, length us, event | category | flops | bytes accessed | tf_op | source)
XLA Modules:
  0.0 162.0 jit_solution(6488589941329140280)
XLA Ops:
  2.3 8.3 %all-to-all-start = ((f32[32,1,128]{2,1,0:T(1,128)}), f32[32,1,128]{2,1,0:T(1,128)S(1)}, u32[]{:S(2)}, u32[]{:S(2)}) async-start(f32[32,1,128]{2,1,0:T(1,128)} %broadcast_in_dim.52), calls=%async_computation | async-start | bytes 32768 | tf_op jit(solution)/shard_map/all_to_all | solution.py:727
  14.5 3.4 %all-to-all-done = f32[32,1,128]{2,1,0:T(1,128)S(1)} async-done(((f32[32,1,128]{2,1,0:T(1,128)}), f32[32,1,128]{2,1,0:T(1,128)S(1)}, u32[]{:S(2)}, u32[]{:S(2)}) %all-to-all-start) | async-done | bytes 16416 | tf_op jit(solution)/shard_map/all_to_all | solution.py:727
  18.3 1.8 %enter.1 = (f32[64,3072]{1,0:T(8,128)S(1)}, bf16[64,4096]{1,0:T(8,128)(2,1)S(1)}, f32[64,64]{1,0:T(8,128)S(1)}, bf16[64,64]{1,0:T(8,128)(2,1)S(1)}) custom-call(bf16[16,2,4,64]{3,2,1,0:T(4,128)(2,1)} %bitcast.44, bf16[16,2,4,64]{3,2,1,0:T(4,128)(2,1)} %bitcast.45, f32[2,64]{1,0:T(2,128)} %gain_hbm.1, bf16[3,128,1024]{2,1,0:T(8,128)(2,1)} %bitcast.42, ...), custom_call_target="tpu_custom_call" | custom-call | tf_op jit(solution)/shard_map/enter/pallas_call | solution.py:161
  21.2 1.5 collective-permute-done.6.refs_5_
  25.0 15.4 %all_to_all.45.spread_ref = bf16[16,4,4096]{2,1,0:T(4,128)(2,1)S(1)} all-to-all(bf16[16,4,4096]{2,1,0:T(4,128)(2,1)S(1)} %reshape.125), channel_id=1, replica_groups={{0,8,16,24,32,40,48,56,64,72,80,88,96,104,112,120},{4,12,20,28,36,44,52..., dimensions={0} | all-to-all | bytes 1048576 | tf_op jit(solution)/shard_map/all_to_all | solution.py:222
  40.7 11.9 %all_to_all.46 = bf16[32,4,1024]{2,1,0:T(4,128)(2,1)S(1)} all-to-all(bf16[32,4,1024]{2,1,0:T(4,128)(2,1)S(1)} %broadcast_in_dim.107), channel_id=1, replica_groups=mesh['seq'=32,'tp'=4] {'seq'}, dimensions={0} | all-to-all | bytes 524288 | tf_op jit(solution)/shard_map/all_to_all | solution.py:286
  52.6 3.9 %cache_attention.1 = bf16[128,1152]{1,0:T(8,128)(2,1)S(1)} custom-call(s32[128,128]{1,0:T(8,128)S(1)} %broadcast_in_dim.100.group_ref, s32[128,128]{1,0:T(8,128)S(1)} %broadcast_in_dim.103.limit_ref, bf16[128,1024]{1,0:T(8,128)(2,1)S(1)} %reshape.126.query_ref, bf16[8,128,1024]{2,1,0:T(8,128)(2,1)} %key_hbm.1, bf16[8,128,1024]{2,1,0:T(8,128)(2,1)} %value_hbm.1), custom_call_target="tpu_custom_call" | custom-call | tf_op jit(solution)/shard_map/cache_attention/pallas_call | solution.py:419
  56.7 12.9 %all_to_all.47.spread_ref = bf16[32,4,1152]{2,1,0:T(4,128)(2,1)S(1)} all-to-all(bf16[32,4,1152]{2,1,0:T(4,128)(2,1)S(1)} %reshape.127), channel_id=1, replica_groups=mesh['seq'=32,'tp'=4] {'seq'}, dimensions={0} | all-to-all | bytes 589824 | tf_op jit(solution)/shard_map/all_to_all | solution.py:785
  70.5 11.3 %all_to_all.48 = bf16[16,4,1024]{2,1,0:T(4,128)(2,1)S(1)} all-to-all(bf16[16,4,1024]{2,1,0:T(4,128)(2,1)S(1)} %broadcast_in_dim.108), channel_id=1, replica_groups={{0,8,16,24,32,40,48,56,64,72,80,88,96,104,112,120},{4,12,20,28,36,44,52..., dimensions={0} | all-to-all | bytes 262144 | tf_op jit(solution)/shard_map/all_to_all | solution.py:294
  82.0 3.1 %collective-permute-start.10 = (bf16[64,128]{1,0:T(8,128)(2,1)S(1)}, bf16[64,128]{1,0:T(8,128)(2,1)S(1)}, u32[]{:S(2)}, u32[]{:S(2)}) collective-permute-start(bf16[64,128]{1,0:T(8,128)(2,1)S(1)} %convert_element_type.60), channel_id=1, source_target_pairs={{0,3},{1,0},{2,1},{3,2},{4,7},{5,4},{6,5},{7,6},{8,11},{9,8},{10,9... | collective-permute-start | bytes 49160 | tf_op jit(solution)/shard_map/ppermute | solution.py:314
  86.7 1.6 copy.43
  88.3 2.1 %collective-permute-done.8 = bf16[64,128]{1,0:T(8,128)(2,1)S(1)} collective-permute-done((bf16[64,128]{1,0:T(8,128)(2,1)S(1)}, bf16[64,128]{1,0:T(8,128)(2,1)S(1)}, u32[]{:S(2)}, u32[]{:S(2)}) %collective-permute-start.8) | collective-permute-done | bytes 16416 | tf_op jit(solution)/shard_map/ppermute | solution.py:314
  92.1 14.1 %all_to_all.49.spread_ref = bf16[16,4,4352]{2,1,0:T(4,128)(2,1)S(1)} all-to-all(bf16[16,4,4352]{2,1,0:T(4,128)(2,1)} %reshape.129), channel_id=1, replica_groups={{0,8,16,24,32,40,48,56,64,72,80,88,96,104,112,120},{4,12,20,28,36,44,52..., dimensions={0} | all-to-all | bytes 1114112 | tf_op jit(solution)/shard_map/all_to_all | solution.py:222
  107.4 3.7 %all-to-all-start.6 = ((bf16[16,4,2048]{2,1,0:T(4,128)(2,1)}), bf16[16,4,2048]{2,1,0:T(4,128)(2,1)S(1)}, u32[]{:S(2)}, u32[]{:S(2)}) async-start(bf16[16,4,2048]{2,1,0:T(4,128)(2,1)} %broadcast_in_dim.109), calls=%async_computation.6 | async-start | bytes 524288 | tf_op jit(solution)/shard_map/all_to_all | solution.py:294
  112.6 7.2 %all-to-all-done.6 = bf16[16,4,2048]{2,1,0:T(4,128)(2,1)S(1)} async-done(((bf16[16,4,2048]{2,1,0:T(4,128)(2,1)}), bf16[16,4,2048]{2,1,0:T(4,128)(2,1)S(1)}, u32[]{:S(2)}, u32[]{:S(2)}) %all-to-all-start.6) | async-done | bytes 262176 | tf_op jit(solution)/shard_map/all_to_all | solution.py:294
  120.2 1.8 %collective-permute-start.11 = (bf16[64,128]{1,0:T(8,128)(2,1)S(1)}, bf16[64,128]{1,0:T(8,128)(2,1)S(1)}, u32[]{:S(2)}, u32[]{:S(2)}) collective-permute-start(bf16[64,128]{1,0:T(8,128)(2,1)S(1)} %convert_element_type.64), channel_id=1, source_target_pairs={{0,2},{1,3},{2,0},{3,1},{4,6},{5,7},{6,4},{7,5},{8,10},{9,11},{10,... | collective-permute-start | bytes 49160 | tf_op jit(solution)/shard_map/ppermute | solution.py:314
  122.0 3.2 %collective-permute-start.13 = (bf16[64,128]{1,0:T(8,128)(2,1)S(1)}, bf16[64,128]{1,0:T(8,128)(2,1)S(1)}, u32[]{:S(2)}, u32[]{:S(2)}) collective-permute-start(bf16[64,128]{1,0:T(8,128)(2,1)S(1)} %convert_element_type.64), channel_id=1, source_target_pairs={{0,3},{1,0},{2,1},{3,2},{4,7},{5,4},{6,5},{7,6},{8,11},{9,8},{10,9... | collective-permute-start | bytes 49160 | tf_op jit(solution)/shard_map/ppermute | solution.py:314
  125.5 1.4 collective-permute-done.12
  127.3 11.8 %all_to_all.50.spread_ref = bf16[16,4,2304]{2,1,0:T(4,128)(2,1)S(1)} all-to-all(bf16[16,4,2304]{2,1,0:T(4,128)(2,1)S(1)} %reshape.131), channel_id=1, replica_groups={{0,8,16,24,32,40,48,56,64,72,80,88,96,104,112,120},{4,12,20,28,36,44,52..., dimensions={0} | all-to-all | bytes 589824 | tf_op jit(solution)/shard_map/all_to_all | solution.py:222
  140.2 10.9 %all_to_all.51 = bf16[16,4,1152]{2,1,0:T(4,128)(2,1)S(1)} all-to-all(bf16[16,4,1152]{2,1,0:T(4,128)(2,1)S(1)} %broadcast_in_dim.114), channel_id=1, replica_groups={{0,8,16,24,32,40,48,56,64,72,80,88,96,104,112,120},{4,12,20,28,36,44,52..., dimensions={0} | all-to-all | bytes 294912 | tf_op jit(solution)/shard_map/all_to_all | solution.py:294
  151.8 1.5 collective-permute-start.18
  153.3 2.6 %collective-permute-start.19 = (bf16[64,256]{1,0:T(8,128)(2,1)S(1)}, bf16[64,256]{1,0:T(8,128)(2,1)S(1)}, u32[]{:S(2)}, u32[]{:S(2)}) collective-permute-start(bf16[64,256]{1,0:T(8,128)(2,1)S(1)} %fusion), channel_id=1, source_target_pairs={{0,1},{1,2},{2,3},{3,0},{4,5},{5,6},{6,7},{7,4},{8,9},{9,10},{10,1... | collective-permute-start | bytes 98312 | tf_op jit(solution)/shard_map/ppermute | solution.py:314
  156.5 1.4 state_update.1
  158.4 1.4 collective-permute-done.20
  (146 shorter events, 22.7 us)
Async XLA Ops:
  2.3 15.6 %all-to-all-start = ((f32[32,1,128]{2,1,0:T(1,128)}), f32[32,1,128]{2,1,0:T(1,128)S(1)}, u32[]{:S(2)}, u32[]{:S(2)}) async-start(f32[32,1,128]{2,1,0:T(1,128)} %broadcast_in_dim.52), calls=%async_computation | async-start | bytes 32768 | tf_op jit(solution)/shard_map/all_to_all | solution.py:727
  10.6 2.5 %collective-permute-start = (f32[64]{0:T(128)}, f32[64]{0:T(128)S(1)}, u32[]{:S(2)}, u32[]{:S(2)}) collective-permute-start(f32[64]{0:T(128)} %param.37), channel_id=1, source_target_pairs={{0,4},{4,0},{8,12},{12,8},{16,20},{20,16},{24,28},{28,24},{32,36},... | collective-permute-start | bytes 776 | tf_op jit(solution)/shard_map/ppermute | solution.py:23
  10.9 2.8 %collective-permute-start.1 = (f32[64]{0:T(128)}, f32[64]{0:T(128)S(1)}, u32[]{:S(2)}, u32[]{:S(2)}) collective-permute-start(f32[64]{0:T(128)} %param.42), channel_id=1, source_target_pairs={{0,4},{4,0},{8,12},{12,8},{16,20},{20,16},{24,28},{28,24},{32,36},... | collective-permute-start | bytes 776 | tf_op jit(solution)/shard_map/ppermute | solution.py:23
  11.2 12.7 %collective-permute-start.4 = (bf16[2,64,2048]{2,1,0:T(8,128)(2,1)}, bf16[2,64,2048]{2,1,0:T(8,128)(2,1)S(1)}, u32[]{:S(2)}, u32[]{:S(2)}) collective-permute-start(bf16[2,64,2048]{2,1,0:T(8,128)(2,1)} %refs_2_.2), channel_id=1, source_target_pairs={{0,4},{4,0},{8,12},{12,8},{16,20},{20,16},{24,28},{28,24},{32,36},... | collective-permute-start | bytes 1572872 | tf_op jit(solution)/shard_map/ppermute | solution.py:23
  20.1 3.8 %collective-permute-start.2 = (bf16[64,4096]{1,0:T(8,128)(2,1)S(1)}, bf16[64,4096]{1,0:T(8,128)(2,1)S(1)}, u32[]{:S(2)}, u32[]{:S(2)}) collective-permute-start(bf16[64,4096]{1,0:T(8,128)(2,1)S(1)} %get-tuple-element.45), channel_id=1, source_target_pairs={{0,4},{4,0},{8,12},{12,8},{16,20},{20,16},{24,28},{28,24},{32,36},... | collective-permute-start | bytes 1572872 | tf_op jit(solution)/shard_map/ppermute | solution.py:23
  20.2 3.7 %collective-permute-start.7 = (bf16[2048,64]{0,1:T(8,128)(2,1)}, bf16[2048,64]{0,1:T(8,128)(2,1)S(1)}, u32[]{:S(2)}, u32[]{:S(2)}) collective-permute-start(bf16[2048,64]{0,1:T(8,128)(2,1)} %param.41), channel_id=1, source_target_pairs={{0,4},{4,0},{8,12},{12,8},{16,20},{20,16},{24,28},{28,24},{32,36},... | collective-permute-start | bytes 786440 | tf_op jit(solution)/shard_map/ppermute | solution.py:23
  20.7 3.2 %collective-permute-start.5 = (bf16[1024,64]{0,1:T(8,128)(2,1)}, bf16[1024,64]{0,1:T(8,128)(2,1)S(1)}, u32[]{:S(2)}, u32[]{:S(2)}) collective-permute-start(bf16[1024,64]{0,1:T(8,128)(2,1)} %param.36), channel_id=1, source_target_pairs={{0,4},{4,0},{8,12},{12,8},{16,20},{20,16},{24,28},{28,24},{32,36},... | collective-permute-start | bytes 393224 | tf_op jit(solution)/shard_map/ppermute | solution.py:23
  20.8 1.9 %collective-permute-start.6 = (bf16[64,128]{1,0:T(8,128)(2,1)}, bf16[64,128]{1,0:T(8,128)(2,1)S(1)}, u32[]{:S(2)}, u32[]{:S(2)}) collective-permute-start(bf16[64,128]{1,0:T(8,128)(2,1)} %refs_3_.2), channel_id=1, source_target_pairs={{0,4},{4,0},{8,12},{12,8},{16,20},{20,16},{24,28},{28,24},{32,36},... | collective-permute-start | bytes 49160 | tf_op jit(solution)/shard_map/ppermute | solution.py:23
  22.7 1.2 collective-permute-start.3
  82.0 6.3 %collective-permute-start.10 = (bf16[64,128]{1,0:T(8,128)(2,1)S(1)}, bf16[64,128]{1,0:T(8,128)(2,1)S(1)}, u32[]{:S(2)}, u32[]{:S(2)}) collective-permute-start(bf16[64,128]{1,0:T(8,128)(2,1)S(1)} %convert_element_type.60), channel_id=1, source_target_pairs={{0,3},{1,0},{2,1},{3,2},{4,7},{5,4},{6,5},{7,6},{8,11},{9,8},{10,9... | collective-permute-start | bytes 49160 | tf_op jit(solution)/shard_map/ppermute | solution.py:314
  85.1 5.2 %collective-permute-start.8 = (bf16[64,128]{1,0:T(8,128)(2,1)S(1)}, bf16[64,128]{1,0:T(8,128)(2,1)S(1)}, u32[]{:S(2)}, u32[]{:S(2)}) collective-permute-start(bf16[64,128]{1,0:T(8,128)(2,1)S(1)} %convert_element_type.60), channel_id=1, source_target_pairs={{0,2},{1,3},{2,0},{3,1},{4,6},{5,7},{6,4},{7,5},{8,10},{9,11},{10,... | collective-permute-start | bytes 49160 | tf_op jit(solution)/shard_map/ppermute | solution.py:314
  85.8 4.9 %collective-permute-start.9 = (bf16[64,128]{1,0:T(8,128)(2,1)S(1)}, bf16[64,128]{1,0:T(8,128)(2,1)S(1)}, u32[]{:S(2)}, u32[]{:S(2)}) collective-permute-start(bf16[64,128]{1,0:T(8,128)(2,1)S(1)} %convert_element_type.60), channel_id=1, source_target_pairs={{0,1},{1,2},{2,3},{3,0},{4,5},{5,6},{6,7},{7,4},{8,9},{9,10},{10,1... | collective-permute-start | bytes 49160 | tf_op jit(solution)/shard_map/ppermute | solution.py:314
  107.4 12.3 %all-to-all-start.6 = ((bf16[16,4,2048]{2,1,0:T(4,128)(2,1)}), bf16[16,4,2048]{2,1,0:T(4,128)(2,1)S(1)}, u32[]{:S(2)}, u32[]{:S(2)}) async-start(bf16[16,4,2048]{2,1,0:T(4,128)(2,1)} %broadcast_in_dim.109), calls=%async_computation.6 | async-start | bytes 524288 | tf_op jit(solution)/shard_map/all_to_all | solution.py:294
  111.1 14.1 %collective-permute-start.15 = (bf16[2,64,1024]{2,1,0:T(8,128)(2,1)S(1)}, bf16[2,64,1024]{2,1,0:T(8,128)(2,1)S(1)}, u32[]{:S(2)}, u32[]{:S(2)}) collective-permute-start(bf16[2,64,1024]{2,1,0:T(8,128)(2,1)S(1)} %copy-done.5), channel_id=1, source_target_pairs={{0,4},{4,0},{8,12},{12,8},{16,20},{20,16},{24,28},{28,24},{32,36},... | collective-permute-start | bytes 786440 | tf_op jit(solution)/shard_map/ppermute | solution.py:23
  111.4 13.8 %collective-permute-start.17 = (bf16[1024,64]{0,1:T(8,128)(2,1)S(1)}, bf16[1024,64]{0,1:T(8,128)(2,1)S(1)}, u32[]{:S(2)}, u32[]{:S(2)}) collective-permute-start(bf16[1024,64]{0,1:T(8,128)(2,1)S(1)} %copy-done.6), channel_id=1, source_target_pairs={{0,4},{4,0},{8,12},{12,8},{16,20},{20,16},{24,28},{28,24},{32,36},... | collective-permute-start | bytes 393224 | tf_op jit(solution)/shard_map/ppermute | solution.py:23
  111.9 10.1 %collective-permute-start.16 = (bf16[64,128]{1,0:T(8,128)(2,1)S(1)}, bf16[64,128]{1,0:T(8,128)(2,1)S(1)}, u32[]{:S(2)}, u32[]{:S(2)}) collective-permute-start(bf16[64,128]{1,0:T(8,128)(2,1)S(1)} %copy-done.12), channel_id=1, source_target_pairs={{0,4},{4,0},{8,12},{12,8},{16,20},{20,16},{24,28},{28,24},{32,36},... | collective-permute-start | bytes 49160 | tf_op jit(solution)/shard_map/ppermute | solution.py:23
  112.1 9.9 %collective-permute-start.14 = (bf16[64,16]{1,0:T(8,128)(2,1)S(1)}, bf16[64,16]{1,0:T(8,128)(2,1)S(1)}, u32[]{:S(2)}, u32[]{:S(2)}) collective-permute-start(bf16[64,16]{1,0:T(8,128)(2,1)S(1)} %copy.39), channel_id=1, source_target_pairs={{0,4},{4,0},{8,12},{12,8},{16,20},{20,16},{24,28},{28,24},{32,36},... | collective-permute-start | bytes 6152 | tf_op jit(solution)/shard_map/ppermute | solution.py:23
  120.2 5.3 %collective-permute-start.11 = (bf16[64,128]{1,0:T(8,128)(2,1)S(1)}, bf16[64,128]{1,0:T(8,128)(2,1)S(1)}, u32[]{:S(2)}, u32[]{:S(2)}) collective-permute-start(bf16[64,128]{1,0:T(8,128)(2,1)S(1)} %convert_element_type.64), channel_id=1, source_target_pairs={{0,2},{1,3},{2,0},{3,1},{4,6},{5,7},{6,4},{7,5},{8,10},{9,11},{10,... | collective-permute-start | bytes 49160 | tf_op jit(solution)/shard_map/ppermute | solution.py:314
  122.0 5.0 %collective-permute-start.12 = (bf16[64,128]{1,0:T(8,128)(2,1)S(1)}, bf16[64,128]{1,0:T(8,128)(2,1)S(1)}, u32[]{:S(2)}, u32[]{:S(2)}) collective-permute-start(bf16[64,128]{1,0:T(8,128)(2,1)S(1)} %convert_element_type.64), channel_id=1, source_target_pairs={{0,1},{1,2},{2,3},{3,0},{4,5},{5,6},{6,7},{7,4},{8,9},{9,10},{10,1... | collective-permute-start | bytes 49160 | tf_op jit(solution)/shard_map/ppermute | solution.py:314
  122.0 4.9 %collective-permute-start.13 = (bf16[64,128]{1,0:T(8,128)(2,1)S(1)}, bf16[64,128]{1,0:T(8,128)(2,1)S(1)}, u32[]{:S(2)}, u32[]{:S(2)}) collective-permute-start(bf16[64,128]{1,0:T(8,128)(2,1)S(1)} %convert_element_type.64), channel_id=1, source_target_pairs={{0,3},{1,0},{2,1},{3,2},{4,7},{5,4},{6,5},{7,6},{8,11},{9,8},{10,9... | collective-permute-start | bytes 49160 | tf_op jit(solution)/shard_map/ppermute | solution.py:314
  151.8 6.2 %collective-permute-start.18 = (bf16[64,256]{1,0:T(8,128)(2,1)S(1)}, bf16[64,256]{1,0:T(8,128)(2,1)S(1)}, u32[]{:S(2)}, u32[]{:S(2)}) collective-permute-start(bf16[64,256]{1,0:T(8,128)(2,1)S(1)} %fusion), channel_id=1, source_target_pairs={{0,2},{1,3},{2,0},{3,1},{4,6},{5,7},{6,4},{7,5},{8,10},{9,11},{10,... | collective-permute-start | bytes 98312 | tf_op jit(solution)/shard_map/ppermute | solution.py:314
  153.3 5.1 %collective-permute-start.19 = (bf16[64,256]{1,0:T(8,128)(2,1)S(1)}, bf16[64,256]{1,0:T(8,128)(2,1)S(1)}, u32[]{:S(2)}, u32[]{:S(2)}) collective-permute-start(bf16[64,256]{1,0:T(8,128)(2,1)S(1)} %fusion), channel_id=1, source_target_pairs={{0,1},{1,2},{2,3},{3,0},{4,5},{5,6},{6,7},{7,4},{8,9},{9,10},{10,1... | collective-permute-start | bytes 98312 | tf_op jit(solution)/shard_map/ppermute | solution.py:314
  155.9 3.9 %collective-permute-start.20 = (bf16[64,256]{1,0:T(8,128)(2,1)S(1)}, bf16[64,256]{1,0:T(8,128)(2,1)S(1)}, u32[]{:S(2)}, u32[]{:S(2)}) collective-permute-start(bf16[64,256]{1,0:T(8,128)(2,1)S(1)} %fusion), channel_id=1, source_target_pairs={{0,3},{1,0},{2,1},{3,2},{4,7},{5,4},{6,5},{7,6},{8,11},{9,8},{10,9... | collective-permute-start | bytes 98312 | tf_op jit(solution)/shard_map/ppermute | solution.py:314
  160.2 1.2 collective-permute-start.21
  (26 other events, 703.4 us)

commit v2 on v1

--- a/solution.py
+++ b/solution.py
@@ -731,18 +731,11 @@
         0,
         tiled=True,
     )
-    early = swap_all(
-        (
-            gate_up_weight,
-            attention_output_weight,
-            adapter_down_weight,
-            middle_norm_gain,
-            mamba_norm_gain,
-            down_weight,
-        ),
-    )
-    middle_gain = jnp.concatenate([middle_norm_gain, early[3]])[None]
-    mamba_gain = jnp.concatenate([mamba_norm_gain, early[4]])[None]
+    gate_up_partner, middle_gain_partner, mamba_gain_partner = swap_all(
+        (gate_up_weight, middle_norm_gain, mamba_norm_gain)
+    )
+    middle_gain = jnp.concatenate([middle_norm_gain, middle_gain_partner])[None]
+    mamba_gain = jnp.concatenate([mamba_norm_gain, mamba_gain_partner])[None]
     stats, group_of, limit, middle_gain, mamba_gain = lax.optimization_barrier(
         (stats, group_of, limit, middle_gain, mamba_gain)
     )
@@ -755,40 +748,36 @@
         qkv_weight,
         jnp.broadcast_to(factor[:, None], (rows, 2 * columns)),
     )
-    (
-        received,
-        hidden_partner,
-        gate_up_partner,
-        output_partner,
-        adapter_down_partner,
-        down_partner,
-    ) = lax.optimization_barrier(
-        (
-            core_swap(from_other),
-            core_swap(hidden_other),
-            early[0],
-            early[1],
-            early[2],
-            early[5],
-        )
-    )
-    hidden_rows = jnp.concatenate([hidden_mine, hidden_partner.astype(F32)], axis=1)
-    part, hidden_rows = lax.optimization_barrier(
-        (merge(from_mine, received, width_local), hidden_rows)
-    )
+    received, gate_up_partner = lax.optimization_barrier(
+        (core_swap(from_other), gate_up_partner)
+    )
+    part = merge(from_mine, received, width_local)
     spread = spread_rows(part, new_tok)
     own_qkv = finish_projection(spread, width_local)
     query = gather_rows(own_qkv[:, :width_local]).reshape(rows, width_local)
+    query, *to_swap = lax.optimization_barrier(
+        (
+            query,
+            hidden_other,
+            attention_output_weight,
+        )
+    )
+    hidden_partner, *partners = swap_all(to_swap)
+    hidden_rows = jnp.concatenate([hidden_mine, hidden_partner.astype(F32)], axis=1)
     pieces = attention_partials(query, prompt_key_cache, prompt_value_cache, group_of, limit)
+    pieces, hidden_rows, partners = lax.optimization_barrier((pieces, hidden_rows, partners))
+    (output_partner,) = partners
     pieces = pieces.reshape(requests, new_tok, width_local + HD)
     own_attn = combine_partials(
         lax.all_to_all(pieces, "seq", 0, 0, tiled=True), own_qkv
     )
     attn = gather_core_rows(own_attn)
-    summed, adapter_up = tp_total(
+    wide = swap_all((down_weight, adapter_down_weight))
+    summed, beside = tp_total(
         chip_product(attn, attention_output_weight, output_partner),
-        jnp.transpose(adapter_up_weight, (1, 0, 2)),
-    )
+        (jnp.transpose(adapter_up_weight, (1, 0, 2)), wide),
+    )
+    adapter_up, (down_partner, adapter_down_partner) = beside
     resid = hidden_rows + summed
 
     spread = spread_rows(
@@ -863,9 +852,7 @@
         ],
         axis=1,
     )
-    both, updated_state = tp_total(
-        jnp.concatenate([product, addends], axis=1), updated_state
-    )
+    both, updated_state = tp_total(jnp.concatenate([product, addends], axis=1), updated_state)
     gated_stat = both[:, 2 * columns : 3 * columns] + both[:, 3 * columns :]
     gated_stat = jnp.concatenate([gated_stat, gated_stat], axis=1)
     inner_width = inner_local * lax.axis_size("tp")

time: 164 us -> 164 us (level)
  blocking collectives: 88.3 us -> 64.7 us
  waiting for transfers between devices: 20.2 us -> 34.3 us
  starting transfers between devices: 29.8 us -> 37.4 us
  local copies, waits for them, and re-layouts: 7.03 us -> 10.1 us
    all_to_all x1 -> x0, blocking collectives: 12.9 us -> none  [on_device(): lax.all_to_all(pieces, 'seq', 0, 0, tiled=True)]
    all_to_all x2 -> x1, blocking collectives: 22.2 us -> 10.9 us  [gather_core_rows(): lax.all_to_all(full, 'seq', 0, 0, axis_index_groups=groups, tiled=True)]
    all_to_all x0 -> x1, waiting for transfers between devices: none -> 8.79 us  [on_device(): lax.all_to_all(pieces, 'seq', 0, 0, tiled=True)]
    all_to_all x1 -> x2, waiting for transfers between devices: 7.18 us -> 14.8 us  [gather_core_rows(): lax.all_to_all(full, 'seq', 0, 0, axis_index_groups=groups, tiled=True)]
    all_to_all x0 -> x1, starting transfers between devices: none -> 4 us  [on_device(): lax.all_to_all(pieces, 'seq', 0, 0, tiled=True)]
    all_to_all x1 -> x2, starting transfers between devices: 3.68 us -> 7.19 us  [gather_core_rows(): lax.all_to_all(full, 'seq', 0, 0, axis_index_groups=groups, tiled=True)]
    unnamed x54 -> x46, local copies, waits for them, and re-layouts: 1.81 us -> 3.52 us
    ppermute x9, waiting for transfers between devices: 5.93 us -> 4.24 us  [tp_total(): parts.append(lax.ppermute(narrow, 'tp', pairs))]
  transfers between devices with their start and end apart: 24 -> 26, of which waited for: 11 -> 11; matrix products, arithmetic and copies ran while one was open for 3% -> 4% of each run, Pallas kernels for 2% -> 5%
where the time goes in v2:
time: 164 us; the launch traced here: 162 us
  blocking collectives  64.7 us (39%)
  starting transfers between devices  37.4 us (23%)
  waiting for transfers between devices  34.3 us (21%)
  Pallas kernels  10.8 us (7%)
  local copies, waits for them, and re-layouts  10.1 us (6%)
  other arithmetic  3.89 us (2%)
    all_to_all x3, blocking collectives, spread_rows(): lax.all_to_all(part, 'seq', 0, 0, axis_index_groups=groups, tiled=True)  41.9 us
    all_to_all x2, waiting for transfers between devices, gather_core_rows(): lax.all_to_all(full, 'seq', 0, 0, axis_index_groups=groups, tiled=True)  14.8 us
    ppermute x9, starting transfers between devices, tp_total(): parts.append(lax.ppermute(narrow, 'tp', pairs))  14.3 us
    all_to_all x1, blocking collectives, gather_rows(): return lax.all_to_all(full, 'seq', 0, 0, tiled=True)  11.9 us
    all_to_all x1, blocking collectives, gather_core_rows(): lax.all_to_all(full, 'seq', 0, 0, axis_index_groups=groups, tiled=True)  10.9 us
    all_to_all x1, waiting for transfers between devices, on_device(): lax.all_to_all(pieces, 'seq', 0, 0, tiled=True)  8.79 us
    all_to_all x1, starting transfers between devices, on_device(): lax.all_to_all(jnp.broadcast_to(stat.reshape(1, 1, rows), (seq_size, 1, r...  8.27 us
    all_to_all x2, starting transfers between devices, gather_core_rows(): lax.all_to_all(full, 'seq', 0, 0, axis_index_groups=groups, tiled=True)  7.19 us
  transfers between devices with their start and end apart: 26, of which 11 were waited for; matrix products, arithmetic and copies ran while one was open for 4% of the time, Pallas kernels for 5%

profile of v2, /device:TPU:0, one launch (start us, length us, event | category | flops | bytes accessed | tf_op | source)
XLA Modules:
  0.0 162.4 jit_solution(16985578048744681168)
XLA Ops:
  2.3 8.3 %all-to-all-start = ((f32[32,1,128]{2,1,0:T(1,128)}), f32[32,1,128]{2,1,0:T(1,128)S(1)}, u32[]{:S(2)}, u32[]{:S(2)}) async-start(f32[32,1,128]{2,1,0:T(1,128)} %broadcast_in_dim.52), calls=%async_computation | async-start | bytes 32768 | tf_op jit(solution)/shard_map/all_to_all | solution.py:727
  14.5 3.4 %all-to-all-done = f32[32,1,128]{2,1,0:T(1,128)S(1)} async-done(((f32[32,1,128]{2,1,0:T(1,128)}), f32[32,1,128]{2,1,0:T(1,128)S(1)}, u32[]{:S(2)}, u32[]{:S(2)}) %all-to-all-start) | async-done | bytes 16416 | tf_op jit(solution)/shard_map/all_to_all | solution.py:727
  18.3 1.8 %enter.1 = (f32[64,3072]{1,0:T(8,128)S(1)}, bf16[64,4096]{1,0:T(8,128)(2,1)S(1)}, f32[64,64]{1,0:T(8,128)S(1)}, bf16[64,64]{1,0:T(8,128)(2,1)S(1)}) custom-call(bf16[16,2,4,64]{3,2,1,0:T(4,128)(2,1)} %bitcast.44, bf16[16,2,4,64]{3,2,1,0:T(4,128)(2,1)} %bitcast.45, f32[2,64]{1,0:T(2,128)} %gain_hbm.1, bf16[3,128,1024]{2,1,0:T(8,128)(2,1)} %bitcast.42, ...), custom_call_target="tpu_custom_call" | custom-call | tf_op jit(solution)/shard_map/enter/pallas_call | solution.py:161
  20.2 1.9 %collective-permute-done.2.received_ref = bf16[64,4096]{1,0:T(8,128)(2,1)S(1)} collective-permute-done((bf16[64,4096]{1,0:T(8,128)(2,1)S(1)}, bf16[64,4096]{1,0:T(8,128)(2,1)S(1)}, u32[]{:S(2)}, u32[]{:S(2)}) %collective-permute-start.2) | collective-permute-done | bytes 524320 | tf_op jit(solution)/shard_map/ppermute | solution.py:23
  22.4 15.4 %all_to_all.45.spread_ref = bf16[16,4,4096]{2,1,0:T(4,128)(2,1)S(1)} all-to-all(bf16[16,4,4096]{2,1,0:T(4,128)(2,1)S(1)} %reshape.125), channel_id=1, replica_groups={{0,8,16,24,32,40,48,56,64,72,80,88,96,104,112,120},{4,12,20,28,36,44,52..., dimensions={0} | all-to-all | bytes 1048576 | tf_op jit(solution)/shard_map/all_to_all | solution.py:222
  38.0 11.9 %all_to_all.46 = bf16[32,4,1024]{2,1,0:T(4,128)(2,1)S(1)} all-to-all(bf16[32,4,1024]{2,1,0:T(4,128)(2,1)S(1)} %broadcast_in_dim.107), channel_id=1, replica_groups=mesh['seq'=32,'tp'=4] {'seq'}, dimensions={0} | all-to-all | bytes 524288 | tf_op jit(solution)/shard_map/all_to_all | solution.py:286
  50.6 3.9 %cache_attention.1 = bf16[128,1152]{1,0:T(8,128)(2,1)S(1)} custom-call(s32[128,128]{1,0:T(8,128)S(1)} %broadcast_in_dim.100.group_ref, s32[128,128]{1,0:T(8,128)S(1)} %broadcast_in_dim.103.limit_ref, bf16[128,1024]{1,0:T(8,128)(2,1)S(1)} %reshape.126.query_ref, bf16[8,128,1024]{2,1,0:T(8,128)(2,1)} %key_hbm.1, bf16[8,128,1024]{2,1,0:T(8,128)(2,1)} %value_hbm.1), custom_call_target="tpu_custom_call" | custom-call | tf_op jit(solution)/shard_map/cache_attention/pallas_call | solution.py:419
  55.4 4.0 %all-to-all-start.3 = ((bf16[32,4,1152]{2,1,0:T(4,128)(2,1)}), bf16[32,4,1152]{2,1,0:T(4,128)(2,1)S(1)}, u32[]{:S(2)}, u32[]{:S(2)}) async-start(bf16[32,4,1152]{2,1,0:T(4,128)(2,1)} %reshape.127), calls=%async_computation.3 | async-start | bytes 589824 | tf_op jit(solution)/shard_map/all_to_all | solution.py:772
  59.8 8.8 %all-to-all-done.3.spread_ref = bf16[32,4,1152]{2,1,0:T(4,128)(2,1)S(1)} async-done(((bf16[32,4,1152]{2,1,0:T(4,128)(2,1)}), bf16[32,4,1152]{2,1,0:T(4,128)(2,1)S(1)}, u32[]{:S(2)}, u32[]{:S(2)}) %all-to-all-start.3) | async-done | bytes 294944 | tf_op jit(solution)/shard_map/all_to_all | solution.py:772
  70.1 3.5 %all-to-all-start.4 = ((bf16[16,4,1024]{2,1,0:T(4,128)(2,1)}), bf16[16,4,1024]{2,1,0:T(4,128)(2,1)S(1)}, u32[]{:S(2)}, u32[]{:S(2)}) async-start(bf16[16,4,1024]{2,1,0:T(4,128)(2,1)} %broadcast_in_dim.108), calls=%async_computation.4 | async-start | bytes 262144 | tf_op jit(solution)/shard_map/all_to_all | solution.py:294
  74.0 7.6 %all-to-all-done.4 = bf16[16,4,1024]{2,1,0:T(4,128)(2,1)S(1)} async-done(((bf16[16,4,1024]{2,1,0:T(4,128)(2,1)}), bf16[16,4,1024]{2,1,0:T(4,128)(2,1)S(1)}, u32[]{:S(2)}, u32[]{:S(2)}) %all-to-all-start.4) | async-done | bytes 131104 | tf_op jit(solution)/shard_map/all_to_all | solution.py:294
  81.9 3.3 %collective-permute-start.6 = (bf16[64,128]{1,0:T(8,128)(2,1)S(1)}, bf16[64,128]{1,0:T(8,128)(2,1)S(1)}, u32[]{:S(2)}, u32[]{:S(2)}) collective-permute-start(bf16[64,128]{1,0:T(8,128)(2,1)S(1)} %convert_element_type.60), channel_id=1, source_target_pairs={{0,2},{1,3},{2,0},{3,1},{4,6},{5,7},{6,4},{7,5},{8,10},{9,11},{10,... | collective-permute-start | bytes 49160 | tf_op jit(solution)/shard_map/ppermute | solution.py:314
  85.8 2.6 %collective-permute-start.8 = (bf16[64,128]{1,0:T(8,128)(2,1)S(1)}, bf16[64,128]{1,0:T(8,128)(2,1)S(1)}, u32[]{:S(2)}, u32[]{:S(2)}) collective-permute-start(bf16[64,128]{1,0:T(8,128)(2,1)S(1)} %convert_element_type.60), channel_id=1, source_target_pairs={{0,3},{1,0},{2,1},{3,2},{4,7},{5,4},{6,5},{7,6},{8,11},{9,8},{10,9... | collective-permute-start | bytes 49160 | tf_op jit(solution)/shard_map/ppermute | solution.py:314
  88.4 1.6 copy.43
  93.1 14.7 %all_to_all.47.spread_ref = bf16[16,4,4352]{2,1,0:T(4,128)(2,1)S(1)} all-to-all(bf16[16,4,4352]{2,1,0:T(4,128)(2,1)} %reshape.129), channel_id=1, replica_groups={{0,8,16,24,32,40,48,56,64,72,80,88,96,104,112,120},{4,12,20,28,36,44,52..., dimensions={0} | all-to-all | bytes 1114112 | tf_op jit(solution)/shard_map/all_to_all | solution.py:222
  109.1 3.7 %all-to-all-start.6 = ((bf16[16,4,2048]{2,1,0:T(4,128)(2,1)}), bf16[16,4,2048]{2,1,0:T(4,128)(2,1)S(1)}, u32[]{:S(2)}, u32[]{:S(2)}) async-start(bf16[16,4,2048]{2,1,0:T(4,128)(2,1)} %broadcast_in_dim.109), calls=%async_computation.6 | async-start | bytes 524288 | tf_op jit(solution)/shard_map/all_to_all | solution.py:294
  114.2 7.2 %all-to-all-done.6 = bf16[16,4,2048]{2,1,0:T(4,128)(2,1)S(1)} async-done(((bf16[16,4,2048]{2,1,0:T(4,128)(2,1)}), bf16[16,4,2048]{2,1,0:T(4,128)(2,1)S(1)}, u32[]{:S(2)}, u32[]{:S(2)}) %all-to-all-start.6) | async-done | bytes 262176 | tf_op jit(solution)/shard_map/all_to_all | solution.py:294
  122.3 2.4 %collective-permute-start.12 = (bf16[64,128]{1,0:T(8,128)(2,1)S(1)}, bf16[64,128]{1,0:T(8,128)(2,1)S(1)}, u32[]{:S(2)}, u32[]{:S(2)}) collective-permute-start(bf16[64,128]{1,0:T(8,128)(2,1)S(1)} %convert_element_type.64), channel_id=1, source_target_pairs={{0,1},{1,2},{2,3},{3,0},{4,5},{5,6},{6,7},{7,4},{8,9},{9,10},{10,1... | collective-permute-start | bytes 49160 | tf_op jit(solution)/shard_map/ppermute | solution.py:314
  125.6 1.5 collective-permute-done.11
  128.8 11.8 %all_to_all.48.spread_ref = bf16[16,4,2304]{2,1,0:T(4,128)(2,1)S(1)} all-to-all(bf16[16,4,2304]{2,1,0:T(4,128)(2,1)S(1)} %reshape.131), channel_id=1, replica_groups={{0,8,16,24,32,40,48,56,64,72,80,88,96,104,112,120},{4,12,20,28,36,44,52..., dimensions={0} | all-to-all | bytes 589824 | tf_op jit(solution)/shard_map/all_to_all | solution.py:222
  141.7 10.9 %all_to_all.49 = bf16[16,4,1152]{2,1,0:T(4,128)(2,1)S(1)} all-to-all(bf16[16,4,1152]{2,1,0:T(4,128)(2,1)S(1)} %broadcast_in_dim.114), channel_id=1, replica_groups={{0,8,16,24,32,40,48,56,64,72,80,88,96,104,112,120},{4,12,20,28,36,44,52..., dimensions={0} | all-to-all | bytes 294912 | tf_op jit(solution)/shard_map/all_to_all | solution.py:294
  154.1 2.1 %collective-permute-start.19 = (bf16[64,256]{1,0:T(8,128)(2,1)S(1)}, bf16[64,256]{1,0:T(8,128)(2,1)S(1)}, u32[]{:S(2)}, u32[]{:S(2)}) collective-permute-start(bf16[64,256]{1,0:T(8,128)(2,1)S(1)} %fusion), channel_id=1, source_target_pairs={{0,1},{1,2},{2,3},{3,0},{4,5},{5,6},{6,7},{7,4},{8,9},{9,10},{10,1... | collective-permute-start | bytes 98312 | tf_op jit(solution)/shard_map/ppermute | solution.py:314
  157.4 1.4 state_update.1
  160.5 1.2 collective-permute-done.21
  (140 shorter events, 26.4 us)
Async XLA Ops:
  2.3 15.6 %all-to-all-start = ((f32[32,1,128]{2,1,0:T(1,128)}), f32[32,1,128]{2,1,0:T(1,128)S(1)}, u32[]{:S(2)}, u32[]{:S(2)}) async-start(f32[32,1,128]{2,1,0:T(1,128)} %broadcast_in_dim.52), calls=%async_computation | async-start | bytes 32768 | tf_op jit(solution)/shard_map/all_to_all | solution.py:727
  10.6 2.5 %collective-permute-start = (f32[64]{0:T(128)}, f32[64]{0:T(128)S(1)}, u32[]{:S(2)}, u32[]{:S(2)}) collective-permute-start(f32[64]{0:T(128)} %param.37), channel_id=1, source_target_pairs={{0,4},{4,0},{8,12},{12,8},{16,20},{20,16},{24,28},{28,24},{32,36},... | collective-permute-start | bytes 776 | tf_op jit(solution)/shard_map/ppermute | solution.py:23
  10.9 2.8 %collective-permute-start.1 = (f32[64]{0:T(128)}, f32[64]{0:T(128)S(1)}, u32[]{:S(2)}, u32[]{:S(2)}) collective-permute-start(f32[64]{0:T(128)} %param.42), channel_id=1, source_target_pairs={{0,4},{4,0},{8,12},{12,8},{16,20},{20,16},{24,28},{28,24},{32,36},... | collective-permute-start | bytes 776 | tf_op jit(solution)/shard_map/ppermute | solution.py:23
  11.2 9.0 %collective-permute-start.3 = (bf16[2,64,2048]{2,1,0:T(8,128)(2,1)}, bf16[2,64,2048]{2,1,0:T(8,128)(2,1)S(1)}, u32[]{:S(2)}, u32[]{:S(2)}) collective-permute-start(bf16[2,64,2048]{2,1,0:T(8,128)(2,1)} %refs_2_.2), channel_id=1, source_target_pairs={{0,4},{4,0},{8,12},{12,8},{16,20},{20,16},{24,28},{28,24},{32,36},... | collective-permute-start | bytes 1572872 | tf_op jit(solution)/shard_map/ppermute | solution.py:23
  50.0 4.6 %collective-permute-start.5 = (bf16[1024,64]{0,1:T(8,128)(2,1)S(1)}, bf16[1024,64]{0,1:T(8,128)(2,1)S(1)}, u32[]{:S(2)}, u32[]{:S(2)}) collective-permute-start(bf16[1024,64]{0,1:T(8,128)(2,1)S(1)} %copy-done.10), channel_id=1, source_target_pairs={{0,4},{4,0},{8,12},{12,8},{16,20},{20,16},{24,28},{28,24},{32,36},... | collective-permute-start | bytes 393224 | tf_op jit(solution)/shard_map/ppermute | solution.py:23
  50.5 4.1 %collective-permute-start.4 = (bf16[64,64]{1,0:T(8,128)(2,1)S(1)}, bf16[64,64]{1,0:T(8,128)(2,1)S(1)}, u32[]{:S(2)}, u32[]{:S(2)}) collective-permute-start(bf16[64,64]{1,0:T(8,128)(2,1)S(1)} %get-tuple-element.54), channel_id=1, source_target_pairs={{0,4},{4,0},{8,12},{12,8},{16,20},{20,16},{24,28},{28,24},{32,36},... | collective-permute-start | bytes 24584 | tf_op jit(solution)/shard_map/ppermute | solution.py:23
  55.4 13.1 %all-to-all-start.3 = ((bf16[32,4,1152]{2,1,0:T(4,128)(2,1)}), bf16[32,4,1152]{2,1,0:T(4,128)(2,1)S(1)}, u32[]{:S(2)}, u32[]{:S(2)}) async-start(bf16[32,4,1152]{2,1,0:T(4,128)(2,1)} %reshape.127), calls=%async_computation.3 | async-start | bytes 589824 | tf_op jit(solution)/shard_map/all_to_all | solution.py:772
  59.5 30.5 %collective-permute-start.9 = (bf16[2048,64]{0,1:T(8,128)(2,1)S(1)}, bf16[2048,64]{0,1:T(8,128)(2,1)S(1)}, u32[]{:S(2)}, u32[]{:S(2)}) collective-permute-start(bf16[2048,64]{0,1:T(8,128)(2,1)S(1)} %copy-done.4), channel_id=1, source_target_pairs={{0,4},{4,0},{8,12},{12,8},{16,20},{20,16},{24,28},{28,24},{32,36},... | collective-permute-start | bytes 786440 | tf_op jit(solution)/shard_map/ppermute | solution.py:23
  70.1 11.5 %all-to-all-start.4 = ((bf16[16,4,1024]{2,1,0:T(4,128)(2,1)}), bf16[16,4,1024]{2,1,0:T(4,128)(2,1)S(1)}, u32[]{:S(2)}, u32[]{:S(2)}) async-start(bf16[16,4,1024]{2,1,0:T(4,128)(2,1)} %broadcast_in_dim.108), calls=%async_computation.4 | async-start | bytes 262144 | tf_op jit(solution)/shard_map/all_to_all | solution.py:294
  73.6 16.3 %collective-permute-start.10 = (bf16[64,128]{1,0:T(8,128)(2,1)S(1)}, bf16[64,128]{1,0:T(8,128)(2,1)S(1)}, u32[]{:S(2)}, u32[]{:S(2)}) collective-permute-start(bf16[64,128]{1,0:T(8,128)(2,1)S(1)} %copy-done.11), channel_id=1, source_target_pairs={{0,4},{4,0},{8,12},{12,8},{16,20},{20,16},{24,28},{28,24},{32,36},... | collective-permute-start | bytes 49160 | tf_op jit(solution)/shard_map/ppermute | solution.py:23
  81.9 8.8 %collective-permute-start.6 = (bf16[64,128]{1,0:T(8,128)(2,1)S(1)}, bf16[64,128]{1,0:T(8,128)(2,1)S(1)}, u32[]{:S(2)}, u32[]{:S(2)}) collective-permute-start(bf16[64,128]{1,0:T(8,128)(2,1)S(1)} %convert_element_type.60), channel_id=1, source_target_pairs={{0,2},{1,3},{2,0},{3,1},{4,6},{5,7},{6,4},{7,5},{8,10},{9,11},{10,... | collective-permute-start | bytes 49160 | tf_op jit(solution)/shard_map/ppermute | solution.py:314
  85.1 5.6 %collective-permute-start.7 = (bf16[64,128]{1,0:T(8,128)(2,1)S(1)}, bf16[64,128]{1,0:T(8,128)(2,1)S(1)}, u32[]{:S(2)}, u32[]{:S(2)}) collective-permute-start(bf16[64,128]{1,0:T(8,128)(2,1)S(1)} %convert_element_type.60), channel_id=1, source_target_pairs={{0,1},{1,2},{2,3},{3,0},{4,5},{5,6},{6,7},{7,4},{8,9},{9,10},{10,1... | collective-permute-start | bytes 49160 | tf_op jit(solution)/shard_map/ppermute | solution.py:314
  85.8 4.9 %collective-permute-start.8 = (bf16[64,128]{1,0:T(8,128)(2,1)S(1)}, bf16[64,128]{1,0:T(8,128)(2,1)S(1)}, u32[]{:S(2)}, u32[]{:S(2)}) collective-permute-start(bf16[64,128]{1,0:T(8,128)(2,1)S(1)} %convert_element_type.60), channel_id=1, source_target_pairs={{0,3},{1,0},{2,1},{3,2},{4,7},{5,4},{6,5},{7,6},{8,11},{9,8},{10,9... | collective-permute-start | bytes 49160 | tf_op jit(solution)/shard_map/ppermute | solution.py:314
  109.1 12.3 %all-to-all-start.6 = ((bf16[16,4,2048]{2,1,0:T(4,128)(2,1)}), bf16[16,4,2048]{2,1,0:T(4,128)(2,1)S(1)}, u32[]{:S(2)}, u32[]{:S(2)}) async-start(bf16[16,4,2048]{2,1,0:T(4,128)(2,1)} %broadcast_in_dim.109), calls=%async_computation.6 | async-start | bytes 524288 | tf_op jit(solution)/shard_map/all_to_all | solution.py:294
  112.8 12.8 %collective-permute-start.15 = (bf16[2,64,1024]{2,1,0:T(8,128)(2,1)S(1)}, bf16[2,64,1024]{2,1,0:T(8,128)(2,1)S(1)}, u32[]{:S(2)}, u32[]{:S(2)}) collective-permute-start(bf16[2,64,1024]{2,1,0:T(8,128)(2,1)S(1)} %copy-done.5), channel_id=1, source_target_pairs={{0,4},{4,0},{8,12},{12,8},{16,20},{20,16},{24,28},{28,24},{32,36},... | collective-permute-start | bytes 786440 | tf_op jit(solution)/shard_map/ppermute | solution.py:23
  113.0 12.5 %collective-permute-start.17 = (bf16[1024,64]{0,1:T(8,128)(2,1)S(1)}, bf16[1024,64]{0,1:T(8,128)(2,1)S(1)}, u32[]{:S(2)}, u32[]{:S(2)}) collective-permute-start(bf16[1024,64]{0,1:T(8,128)(2,1)S(1)} %copy-done.8), channel_id=1, source_target_pairs={{0,4},{4,0},{8,12},{12,8},{16,20},{20,16},{24,28},{28,24},{32,36},... | collective-permute-start | bytes 393224 | tf_op jit(solution)/shard_map/ppermute | solution.py:23
  113.5 11.2 %collective-permute-start.16 = (bf16[64,128]{1,0:T(8,128)(2,1)S(1)}, bf16[64,128]{1,0:T(8,128)(2,1)S(1)}, u32[]{:S(2)}, u32[]{:S(2)}) collective-permute-start(bf16[64,128]{1,0:T(8,128)(2,1)S(1)} %copy-done.12), channel_id=1, source_target_pairs={{0,4},{4,0},{8,12},{12,8},{16,20},{20,16},{24,28},{28,24},{32,36},... | collective-permute-start | bytes 49160 | tf_op jit(solution)/shard_map/ppermute | solution.py:23
  113.7 8.6 %collective-permute-start.14 = (bf16[64,16]{1,0:T(8,128)(2,1)S(1)}, bf16[64,16]{1,0:T(8,128)(2,1)S(1)}, u32[]{:S(2)}, u32[]{:S(2)}) collective-permute-start(bf16[64,16]{1,0:T(8,128)(2,1)S(1)} %copy.39), channel_id=1, source_target_pairs={{0,4},{4,0},{8,12},{12,8},{16,20},{20,16},{24,28},{28,24},{32,36},... | collective-permute-start | bytes 6152 | tf_op jit(solution)/shard_map/ppermute | solution.py:23
  121.8 5.3 %collective-permute-start.11 = (bf16[64,128]{1,0:T(8,128)(2,1)S(1)}, bf16[64,128]{1,0:T(8,128)(2,1)S(1)}, u32[]{:S(2)}, u32[]{:S(2)}) collective-permute-start(bf16[64,128]{1,0:T(8,128)(2,1)S(1)} %convert_element_type.64), channel_id=1, source_target_pairs={{0,2},{1,3},{2,0},{3,1},{4,6},{5,7},{6,4},{7,5},{8,10},{9,11},{10,... | collective-permute-start | bytes 49160 | tf_op jit(solution)/shard_map/ppermute | solution.py:314
  122.3 5.0 %collective-permute-start.12 = (bf16[64,128]{1,0:T(8,128)(2,1)S(1)}, bf16[64,128]{1,0:T(8,128)(2,1)S(1)}, u32[]{:S(2)}, u32[]{:S(2)}) collective-permute-start(bf16[64,128]{1,0:T(8,128)(2,1)S(1)} %convert_element_type.64), channel_id=1, source_target_pairs={{0,1},{1,2},{2,3},{3,0},{4,5},{5,6},{6,7},{7,4},{8,9},{9,10},{10,1... | collective-permute-start | bytes 49160 | tf_op jit(solution)/shard_map/ppermute | solution.py:314
  124.7 3.7 %collective-permute-start.13 = (bf16[64,128]{1,0:T(8,128)(2,1)S(1)}, bf16[64,128]{1,0:T(8,128)(2,1)S(1)}, u32[]{:S(2)}, u32[]{:S(2)}) collective-permute-start(bf16[64,128]{1,0:T(8,128)(2,1)S(1)} %convert_element_type.64), channel_id=1, source_target_pairs={{0,3},{1,0},{2,1},{3,2},{4,7},{5,4},{6,5},{7,6},{8,11},{9,8},{10,9... | collective-permute-start | bytes 49160 | tf_op jit(solution)/shard_map/ppermute | solution.py:314
  153.3 5.5 %collective-permute-start.18 = (bf16[64,256]{1,0:T(8,128)(2,1)S(1)}, bf16[64,256]{1,0:T(8,128)(2,1)S(1)}, u32[]{:S(2)}, u32[]{:S(2)}) collective-permute-start(bf16[64,256]{1,0:T(8,128)(2,1)S(1)} %fusion), channel_id=1, source_target_pairs={{0,2},{1,3},{2,0},{3,1},{4,6},{5,7},{6,4},{7,5},{8,10},{9,11},{10,... | collective-permute-start | bytes 98312 | tf_op jit(solution)/shard_map/ppermute | solution.py:314
  154.1 5.1 %collective-permute-start.19 = (bf16[64,256]{1,0:T(8,128)(2,1)S(1)}, bf16[64,256]{1,0:T(8,128)(2,1)S(1)}, u32[]{:S(2)}, u32[]{:S(2)}) collective-permute-start(bf16[64,256]{1,0:T(8,128)(2,1)S(1)} %fusion), channel_id=1, source_target_pairs={{0,1},{1,2},{2,3},{3,0},{4,5},{5,6},{6,7},{7,4},{8,9},{9,10},{10,1... | collective-permute-start | bytes 98312 | tf_op jit(solution)/shard_map/ppermute | solution.py:314
  156.2 3.9 %collective-permute-start.20 = (bf16[64,256]{1,0:T(8,128)(2,1)S(1)}, bf16[64,256]{1,0:T(8,128)(2,1)S(1)}, u32[]{:S(2)}, u32[]{:S(2)}) collective-permute-start(bf16[64,256]{1,0:T(8,128)(2,1)S(1)} %fusion), channel_id=1, source_target_pairs={{0,3},{1,0},{2,1},{3,2},{4,7},{5,4},{6,5},{7,6},{8,11},{9,8},{10,9... | collective-permute-start | bytes 98312 | tf_op jit(solution)/shard_map/ppermute | solution.py:314
  (24 other events, 547.1 us)
